TPU v7x, 32 devices: a whole 2x2x4 slice. The times are simulated.
32 devices in a mesh: gx: 4 (over y, x), gy: 8 (over z, core).
Axes of the slice: x: 2, y: 2, z: 4, core: 2. Of those that a mesh axis runs over, the one named last changes fastest.
Arguments:
- tokens: bfloat16 [32, 2048, 768], P(('gx', 'gy')), may hold values from -6 to 6
- cotangent: bfloat16 [32, 2048, 768], P(('gx', 'gy')), may hold values from -6 to 6
- chosen: int32 [32, 256], P(('gx', 'gy')), may hold values from 0 to 2047, as said below
- segment: int32 [32, 2048], P(('gx', 'gy')), may hold values from 0 to 5, never falling along the last dimension, each value on 1 to 1024 neighbouring positions
- router: bfloat16 [768], P(('gx', 'gy')), may hold values from -0.21875 to 0.21875
- gain_one: bfloat16 [768], P(('gx', 'gy')), may hold values from 0.25 to 1.75
- gain_two: bfloat16 [768], P(('gx', 'gy')), may hold values from 0.25 to 1.75
- query_weight: bfloat16 [768, 768], P(('gx', 'gy')), may hold values from -0.21875 to 0.21875
- key_weight: bfloat16 [768, 768], P(('gx', 'gy')), may hold values from -0.21875 to 0.21875
- value_weight: bfloat16 [768, 768], P(('gx', 'gy')), may hold values from -0.21875 to 0.21875
- output_weight: bfloat16 [768, 768], P(('gx', 'gy')), may hold values from -0.875 to 0.875
- expand_weight: bfloat16 [768, 3072], P(('gx', 'gy')), may hold values from -0.21875 to 0.21875
- shrink_weight: bfloat16 [3072, 768], P(('gx', 'gy')), may hold values from -0.109375 to 0.109375
Outputs:
- out_tokens: bfloat16 [32, 2048, 768], P(('gx', 'gy'))
- grad_tokens: bfloat16 [32, 2048, 768], P(('gx', 'gy'))
- grad_router: float32 [768], P(('gx', 'gy'))
- grad_gain_one: float32 [768], P(('gx', 'gy'))
- grad_gain_two: float32 [768], P(('gx', 'gy'))
- grad_query: float32 [768, 768], P(('gx', 'gy'))
- grad_key: float32 [768, 768], P(('gx', 'gy'))
- grad_value: float32 [768, 768], P(('gx', 'gy'))
- grad_output: float32 [768, 768], P(('gx', 'gy'))
- grad_expand: float32 [768, 3072], P(('gx', 'gy'))
- grad_shrink: float32 [3072, 768], P(('gx', 'gy'))
Inputs may be any that keep to these rules, and one draw needn't show every extreme that they name: `chosen`: each row holds 256 different positions of its packed row in increasing order. segment numbers never fall along a row; a segment has at most 1024 positions, one exactly that many.
All inputs are finite; a program needn't handle non-finite values.
Results may differ from a plain program's by a relative error of at most 0.011.
Values may be sent and summed in bfloat16 or wider, within the bound.
No kernel may reach another device: no remote copies, remote signals or barrier semaphores. Data moves between devices by JAX's collectives and lax.ppermute only.
A program may use at most 192 MiB of HBM per device.

v0:
```python
from functools import partial

import jax
import jax.numpy as jnp
from jax import lax
from jax.sharding import PartitionSpec as P

HEAD_DIM = 64


SCALE = 0.125
EPS = 1e-06
NEGATIVE = -1e30


def rms_norm(values, gain):
    return values * lax.rsqrt(jnp.mean(values * values, axis=-1, keepdims=True) + EPS) * gain


def matmul(left, right):
    return jnp.dot(left, right, preferred_element_type=jnp.float32)


def matmul_left_t(left, right):
    return lax.dot_general(
        left, right, (((0,), (0,)), ((), ())), preferred_element_type=jnp.float32
    )


def matmul_right_t(left, right):
    return lax.dot_general(
        left, right, (((1,), (1,)), ((), ())), preferred_element_type=jnp.float32
    )


def body(
    tokens,
    cotangent,
    chosen,
    segment,
    router,
    gain_one,
    gain_two,
    query_weight,
    key_weight,
    value_weight,
    output_weight,
    expand_weight,
    shrink_weight,
):
    attn_full = (
        lax.all_gather(router, ("gx", "gy"), axis=0, tiled=True),
        lax.all_gather(gain_one, ("gx", "gy"), axis=0, tiled=True),
        lax.all_gather(gain_two, ("gx", "gy"), axis=0, tiled=True),
        lax.all_gather(query_weight, ("gx", "gy"), axis=0, tiled=True),
        lax.all_gather(key_weight, ("gx", "gy"), axis=0, tiled=True),
        lax.all_gather(value_weight, ("gx", "gy"), axis=0, tiled=True),
        lax.all_gather(output_weight, ("gx", "gy"), axis=0, tiled=True),
    )
    mlp_full = (
        lax.all_gather(expand_weight, ("gx", "gy"), axis=0, tiled=True),
        lax.all_gather(shrink_weight, ("gx", "gy"), axis=0, tiled=True),
    )
    router_all, gain_one_all, gain_two_all, query_all, key_all, value_all, output_all = attn_full
    expand_all, shrink_all = mlp_full
    row_count, seq_len, width = tokens.shape
    keep_count = chosen.shape[1]
    head_size = HEAD_DIM
    head_count = width // head_size
    token_count = row_count * keep_count
    row_ids = jnp.arange(row_count, dtype=jnp.int32)[:, None]
    hidden_low = tokens[row_ids, chosen].reshape(token_count, width)
    hidden = hidden_low.astype(jnp.float32)
    router_gate = jax.nn.sigmoid(matmul(hidden_low, router_all))
    normed = rms_norm(hidden, gain_one_all.astype(jnp.float32)).astype(jnp.bfloat16)
    head_shape = (row_count, keep_count, head_count, head_size)
    queries = matmul(normed, query_all).astype(jnp.bfloat16).reshape(head_shape)
    key_rows = matmul(normed, key_all).astype(jnp.bfloat16).reshape(head_shape)
    value_rows = matmul(normed, value_all).astype(jnp.bfloat16).reshape(head_shape)
    labels = jnp.take_along_axis(segment, chosen, axis=1)
    allowed = (
        (chosen[:, None, :] <= chosen[:, :, None]) & (labels[:, None, :] == labels[:, :, None])
    )[:, None]

    def attn_scores():
        raw_scores = (
            jnp.einsum("rqhd,rkhd->rhqk", queries, key_rows, preferred_element_type=jnp.float32)
            * SCALE
        )
        return jnp.where(allowed, raw_scores, NEGATIVE)

    scores = attn_scores()
    peak = jnp.max(scores, axis=-1, keepdims=True)
    exp_terms = jnp.exp(scores - peak)
    total_mass = jnp.sum(exp_terms, axis=-1, keepdims=True)
    probs_low = (exp_terms / total_mass).astype(jnp.bfloat16)
    log_mass = peak + jnp.log(total_mass)
    attn_mixed = (
        jnp.einsum("rhqk,rkhd->rqhd", probs_low, value_rows, preferred_element_type=jnp.float32)
        .astype(jnp.bfloat16)
        .reshape(token_count, width)
    )
    attn_out = matmul(attn_mixed, output_all)
    middle = hidden + attn_out
    normed_two = rms_norm(middle, gain_two_all.astype(jnp.float32)).astype(jnp.bfloat16)
    pre_act = matmul(normed_two, expand_all)
    gelu_values, gelu_back = jax.vjp(partial(jax.nn.gelu, approximate=True), pre_act)
    activated = gelu_values.astype(jnp.bfloat16)
    mlp_out = matmul(activated, shrink_all)
    branch = attn_out + mlp_out
    updated = hidden + router_gate[:, None] * branch
    out_tokens = tokens.at[row_ids, chosen].set(
        updated.astype(jnp.bfloat16).reshape(row_count, keep_count, width)
    )
    back_small = (
        lax.all_gather(router, ("gx", "gy"), axis=0, tiled=True),
        lax.all_gather(gain_one, ("gx", "gy"), axis=0, tiled=True),
        lax.all_gather(gain_two, ("gx", "gy"), axis=0, tiled=True),
        lax.all_gather(query_weight, ("gx", "gy"), axis=0, tiled=True),
        lax.all_gather(key_weight, ("gx", "gy"), axis=0, tiled=True),
        lax.all_gather(value_weight, ("gx", "gy"), axis=0, tiled=True),
        lax.all_gather(output_weight, ("gx", "gy"), axis=0, tiled=True),
    )
    back_mlp = (
        lax.all_gather(expand_weight, ("gx", "gy"), axis=0, tiled=True),
        lax.all_gather(shrink_weight, ("gx", "gy"), axis=0, tiled=True),
    )
    router_back, gain_one_back, gain_two_back, query_back, key_back, value_back, output_back = (
        back_small
    )
    expand_back, shrink_back = back_mlp
    cot_rows = cotangent[row_ids, chosen].reshape(token_count, width).astype(jnp.float32)
    grad_branch = router_gate[:, None] * cot_rows
    logit_low = (jnp.sum(cot_rows * branch, axis=-1) * router_gate * (1.0 - router_gate)).astype(
        jnp.bfloat16
    )
    grad_router = matmul(logit_low, hidden_low)
    mlp_low = grad_branch.astype(jnp.bfloat16)
    grad_shrink = matmul_left_t(activated, mlp_low)
    (grad_pre,) = gelu_back(matmul_right_t(mlp_low, shrink_back))
    pre_low = grad_pre.astype(jnp.bfloat16)
    grad_expand = matmul_left_t(normed_two, pre_low)
    grad_normed_two = matmul_right_t(pre_low, expand_back)
    norm_two_value, norm_two_back = jax.vjp(rms_norm, middle, gain_two_back.astype(jnp.float32))
    grad_middle, grad_gain_two = norm_two_back(grad_normed_two)
    attn_low = (grad_middle + grad_branch).astype(jnp.bfloat16)
    grad_output = matmul_left_t(attn_mixed, attn_low)
    mixed_low = matmul_right_t(attn_low, output_back).astype(jnp.bfloat16).reshape(head_shape)
    probs_again = jnp.exp(attn_scores() - log_mass)
    probs_again_low = probs_again.astype(jnp.bfloat16)
    dvalue_low = (
        jnp.einsum(
            "rhqk,rqhd->rkhd", probs_again_low, mixed_low, preferred_element_type=jnp.float32
        )
        .astype(jnp.bfloat16)
        .reshape(token_count, width)
    )
    grad_probs = jnp.einsum(
        "rqhd,rkhd->rhqk", mixed_low, value_rows, preferred_element_type=jnp.float32
    )
    scores_low = (
        probs_again * (grad_probs - jnp.sum(probs_again * grad_probs, axis=-1, keepdims=True))
    ).astype(jnp.bfloat16)
    dquery_low = (
        (
            jnp.einsum("rhqk,rkhd->rqhd", scores_low, key_rows, preferred_element_type=jnp.float32)
            * SCALE
        )
        .astype(jnp.bfloat16)
        .reshape(token_count, width)
    )
    dkey_low = (
        (
            jnp.einsum("rhqk,rqhd->rkhd", scores_low, queries, preferred_element_type=jnp.float32)
            * SCALE
        )
        .astype(jnp.bfloat16)
        .reshape(token_count, width)
    )
    grad_query = matmul_left_t(normed, dquery_low)
    grad_key = matmul_left_t(normed, dkey_low)
    grad_value = matmul_left_t(normed, dvalue_low)
    grad_normed = (
        matmul_right_t(dquery_low, query_back)
        + matmul_right_t(dkey_low, key_back)
        + matmul_right_t(dvalue_low, value_back)
    )
    norm_one_value, norm_one_back = jax.vjp(rms_norm, hidden, gain_one_back.astype(jnp.float32))
    norm_back, grad_gain_one = norm_one_back(grad_normed)
    grad_hidden = (
        cot_rows
        + grad_middle
        + norm_back
        + logit_low.astype(jnp.float32)[:, None] * router_back.astype(jnp.float32)[None, :]
    )
    grad_tokens = cotangent.at[row_ids, chosen].set(
        grad_hidden.astype(jnp.bfloat16).reshape(row_count, keep_count, width)
    )
    shares = tuple(
        (
            lax.psum_scatter(grad_router, ("gx", "gy"), scatter_dimension=0, tiled=True),
            lax.psum_scatter(grad_gain_one, ("gx", "gy"), scatter_dimension=0, tiled=True),
            lax.psum_scatter(grad_gain_two, ("gx", "gy"), scatter_dimension=0, tiled=True),
            lax.psum_scatter(grad_query, ("gx", "gy"), scatter_dimension=0, tiled=True),
            lax.psum_scatter(grad_key, ("gx", "gy"), scatter_dimension=0, tiled=True),
            lax.psum_scatter(grad_value, ("gx", "gy"), scatter_dimension=0, tiled=True),
            lax.psum_scatter(grad_output, ("gx", "gy"), scatter_dimension=0, tiled=True),
            lax.psum_scatter(grad_expand, ("gx", "gy"), scatter_dimension=0, tiled=True),
            lax.psum_scatter(grad_shrink, ("gx", "gy"), scatter_dimension=0, tiled=True),
        )
    )
    return (
        out_tokens,
        grad_tokens,
        shares[0],
        shares[1],
        shares[2],
        shares[3],
        shares[4],
        shares[5],
        shares[6],
        shares[7],
        shares[8],
    )


def solution(mesh):
    in_specs = (
        P(("gx", "gy"), None, None),
        P(("gx", "gy"), None, None),
        P(("gx", "gy"), None),
        P(("gx", "gy"), None),
        P(("gx", "gy")),
        P(("gx", "gy")),
        P(("gx", "gy")),
        P(("gx", "gy"), None),
        P(("gx", "gy"), None),
        P(("gx", "gy"), None),
        P(("gx", "gy"), None),
        P(("gx", "gy"), None),
        P(("gx", "gy"), None),
    )
    out_specs = (
        P(("gx", "gy"), None, None),
        P(("gx", "gy"), None, None),
        P(("gx", "gy")),
        P(("gx", "gy")),
        P(("gx", "gy")),
        P(("gx", "gy"), None),
        P(("gx", "gy"), None),
        P(("gx", "gy"), None),
        P(("gx", "gy"), None),
        P(("gx", "gy"), None),
        P(("gx", "gy"), None),
    )
    return jax.shard_map(body, mesh=mesh, in_specs=in_specs, out_specs=out_specs, check_vma=False)
```

profile of v0, /device:TPU:0, one launch (start us, length us, event | category | flops | bytes accessed | tf_op | source)
XLA Modules:
  0.0 1086.2 jit_solution(10091907107130305303)
XLA Ops:
  7.2 3.9 copy.63
  15.4 42.1 %all-reduce.8 = (bf16[768]{0:T(1024)(128)(2,1)S(1)}, bf16[768]{0:T(1024)(128)(2,1)S(1)}, bf16[768]{0:T(1024)(128)(2,1)S(1)}) all-reduce(bf16[768]{0:T(1024)(128)(2,1)S(1)} %dynamic-update-slice.1, bf16[768]{0:T(1024)(128)(2,1)S(1)} %dynamic-update-slice.2, bf16[768]{0:T(1024)(128)(2,1)S(1)} %dynamic-update-slice), channel_id=1, replica_groups=mesh['gx'=4,'gy'=8] {'gx','gy'}, use_global_device_ids=true, to_apply=%add.2 | all-reduce | flops 2304 | bytes 9216
  59.3 3.0 gather_fusion
  62.4 2.9 gather_fusion.2
  65.9 1.7 gather_fusion.1
  68.6 1.5 compare_and_fusion
  70.1 1.5 fusion.64
  71.6 1.8 convolution_convert_fusion.2
  73.4 0.9 copy.45
  74.3 50.2 %all-gather.11.cloned.1.call-done = bf16[768,768]{1,0:T(8,128)(2,1)} async-done(((bf16[24,768]{1,0:T(8,128)(2,1)}), bf16[768,768]{1,0:T(8,128)(2,1)}) %all-gather.11.cloned.1.call-update) | async-done | bytes 1179664 | tf_op jit(solution)/shard_map/all_gather | solution.py:56
  124.6 1.8 convolution_convert_fusion.1
  126.4 0.9 copy.46
  127.3 53.3 %all-gather.7.cloned.1.call-done = bf16[768,768]{1,0:T(8,128)(2,1)} async-done(((bf16[24,768]{1,0:T(8,128)(2,1)}), bf16[768,768]{1,0:T(8,128)(2,1)}) %all-gather.7.cloned.1.call-update) | async-done | bytes 1179664 | tf_op jit(solution)/shard_map/all_gather | solution.py:57
  180.6 1.8 convolution_convert_fusion.3
  182.4 0.9 copy.44
  183.4 1.8 fusion.63
  186.3 1.4 fusion.13
  187.7 48.8 %all-gather.13.cloned.1.call-done = bf16[768,768]{1,0:T(8,128)(2,1)} async-done(((bf16[24,768]{1,0:T(8,128)(2,1)}), bf16[768,768]{1,0:T(8,128)(2,1)}) %all-gather.13.cloned.1.call-update) | async-done | bytes 1179664 | tf_op jit(solution)/shard_map/all_gather | solution.py:58
  236.5 3.1 multiply_reduce_fusion.3
  240.2 61.8 %all-gather.15.cloned.1.call-done = bf16[768,3072]{1,0:T(8,128)(2,1)} async-done(((bf16[24,3072]{1,0:T(8,128)(2,1)}), bf16[768,3072]{1,0:T(8,128)(2,1)}) %all-gather.15.cloned.1.call-update) | async-done | bytes 4718608 | tf_op jit(solution)/shard_map/all_gather | solution.py:61
  301.9 5.8 fusion.52
  307.7 59.1 %all-gather.17.cloned.1.call-done = bf16[3072,768]{1,0:T(8,128)(2,1)} async-done(((bf16[96,768]{1,0:T(8,128)(2,1)}), bf16[3072,768]{1,0:T(8,128)(2,1)}) %all-gather.17.cloned.1.call-update) | async-done | bytes 4718608 | tf_op jit(solution)/shard_map/all_gather | solution.py:62
  366.8 6.6 fusion.29
  374.0 4.1 fusion.6
  378.2 2.2 multiply_reduce_fusion.1
  382.0 1.9 fusion.66
  384.0 1.4 log_add_fusion
  385.3 2.7 convolution_convert_fusion
  388.0 1.9 copy.48
  389.9 1.6 fusion.14
  392.3 2.1 fusion.53
  394.5 2.0 multiply_reduce_fusion
  397.2 1.2 copy-done.6
  399.7 2.1 fusion.55
  403.0 2.0 fusion.57
  405.1 6.9 fusion.43
  413.7 5.2 fusion.51
  421.7 1.8 fusion.65
  424.2 1.5 fusion.24
  425.7 39.7 %all-reduce.7 = (f32[768]{0:T(1024)S(1)}, f32[768]{0:T(1024)S(1)}, f32[768]{0:T(1024)S(1)}) all-reduce(f32[768]{0:T(1024)S(1)} %copy-done.41, f32[768]{0:T(1024)S(1)} %get-tuple-element.13, f32[768]{0:T(1024)S(1)} %copy-done.52), channel_id=2, replica_groups=mesh['gx'=4,'gy'=8] {'gx','gy'}, use_global_device_ids=true, to_apply=%region_10.11.clone | all-reduce | flops 2304 | bytes 18432
  467.2 6.4 scatter_custom_fusion
  473.6 6.3 scatter_custom_fusion.1
  479.9 2.7 reduce-scatter.13.cloned.1.call-done
  482.6 104.5 %reduce-scatter.11.cloned.1.call-done = f32[24,768]{1,0:T(8,128)} async-done(((f32[768,768]{1,0:T(8,128)}), f32[24,768]{1,0:T(8,128)}) %reduce-scatter.11.cloned.1.call-update) | async-done | bytes 73744 | tf_op jit(solution)/shard_map/reduce_scatter | solution.py:206
  587.1 104.4 %reduce-scatter.9.cloned.1.call-done = f32[24,768]{1,0:T(8,128)} async-done(((f32[768,768]{1,0:T(8,128)}), f32[24,768]{1,0:T(8,128)}) %reduce-scatter.9.cloned.1.call-update) | async-done | bytes 73744 | tf_op jit(solution)/shard_map/reduce_scatter | solution.py:205
  691.5 104.3 %reduce-scatter.7.cloned.1.call-done = f32[24,768]{1,0:T(8,128)} async-done(((f32[768,768]{1,0:T(8,128)}), f32[24,768]{1,0:T(8,128)}) %reduce-scatter.7.cloned.1.call-update) | async-done | bytes 73744 | tf_op jit(solution)/shard_map/reduce_scatter | solution.py:204
  795.8 142.0 %reduce-scatter.17.cloned.1.call-done = f32[96,768]{1,0:T(8,128)} async-done(((f32[3072,768]{1,0:T(8,128)}), f32[96,768]{1,0:T(8,128)}) %reduce-scatter.17.cloned.1.call-update) | async-done | bytes 294928 | tf_op jit(solution)/shard_map/reduce_scatter | solution.py:209
  937.8 141.5 %reduce-scatter.15.cloned.1.call-done = f32[24,3072]{1,0:T(8,128)} async-done(((f32[768,3072]{1,0:T(8,128)}), f32[24,3072]{1,0:T(8,128)}) %reduce-scatter.15.cloned.1.call-update) | async-done | bytes 294928 | tf_op jit(solution)/shard_map/reduce_scatter | solution.py:208
  (179 shorter events, 22.3 us)
Async XLA Ops:
  7.2 58.8 %copy-start = (s32[1,2048]{1,0:T(1,128)S(1)}, s32[1,2048]{1,0:T(1,128)}, u32[]{:S(2)}) copy-start(s32[1,2048]{1,0:T(1,128)} %param.16) | copy-start | bytes 24580
  7.2 64.4 %all-gather.9.cloned.1.call-start = ((), (), s32[]{:S(2)}) async-start(), calls=%async_computation.7 | async-start | bytes 1216512 | tf_op jit(solution)/shard_map/all_gather | solution.py:55
  7.2 3.9 copy-start.20
  11.2 3.6 copy-start.55
  11.2 3.8 copy-start.56
  11.2 4.0 copy-start.57
  11.2 47.6 %copy-start.38 = (s32[1,256]{1,0:T(1,128)S(1)}, s32[1,256]{1,0:T(1,128)}, u32[]{:S(2)}) copy-start(s32[1,256]{1,0:T(1,128)} %param.15) | copy-start | bytes 3076
  11.4 53.9 %copy-start.8 = (bf16[1,2048,768]{2,1,0:T(8,128)(2,1)}, bf16[1,2048,768]{2,1,0:T(8,128)(2,1)S(1)}, u32[]{:S(2)}) copy-start(bf16[1,2048,768]{2,1,0:T(8,128)(2,1)S(1)} %copy.64) | copy-start | bytes 9437188
  11.4 113.1 %all-gather.11.cloned.1.call-start = ((), (), s32[]{:S(2)}) async-start(), calls=%async_computation.8 | async-start | bytes 1216512 | tf_op jit(solution)/shard_map/all_gather | solution.py:56
  12.2 168.4 %all-gather.7.cloned.1.call-start = ((), (), s32[]{:S(2)}) async-start(), calls=%async_computation.6 | async-start | bytes 1216512 | tf_op jit(solution)/shard_map/all_gather | solution.py:57
  12.9 223.6 %all-gather.13.cloned.1.call-start = ((), (), s32[]{:S(2)}) async-start(), calls=%async_computation.9 | async-start | bytes 1216512 | tf_op jit(solution)/shard_map/all_gather | solution.py:58
  13.5 288.4 %all-gather.15.cloned.1.call-start = ((), (), s32[]{:S(2)}) async-start(), calls=%async_computation.10 | async-start | bytes 4866048 | tf_op jit(solution)/shard_map/all_gather | solution.py:61
  14.1 352.7 %all-gather.17.cloned.1.call-start = ((), (), s32[]{:S(2)}) async-start(), calls=%async_computation.11 | async-start | bytes 4866048 | tf_op jit(solution)/shard_map/all_gather | solution.py:62
  14.7 467.9 %reduce-scatter.13.cloned.1.call-start = ((), (), s32[]{:S(2)}) async-start(), calls=%async_computation.15 | async-start | bytes 2433024 | tf_op jit(solution)/shard_map/reduce_scatter | solution.py:207
  65.9 58.6 %copy-start.32 = (f32[768]{0:T(1024)S(1)}, f32[768]{0:T(1024)}, u32[]{:S(2)}) copy-start(f32[768]{0:T(1024)} %convert_element_type.147) | copy-start | bytes 9220
  67.8 59.5 %copy-start.43 = (f32[256]{0:T(256)}, f32[256]{0:T(256)S(1)}, u32[]{:S(2)}) copy-start(f32[256]{0:T(256)S(1)} %fusion.30) | copy-start | bytes 3076
  67.9 356.2 %copy-start.36 = (f32[256]{0:T(256)}, f32[256]{0:T(256)S(1)}, u32[]{:S(2)}) copy-start(f32[256]{0:T(256)S(1)} %fusion.49) | copy-start | bytes 3076
  183.4 2.9 copy-start.26
  240.2 172.1 %copy-start.34 = (f32[256]{0:T(256)}, f32[256]{0:T(256)S(1)}, u32[]{:S(2)}) copy-start(f32[256]{0:T(256)S(1)} %fusion.50) | copy-start | bytes 3076
  366.8 6.6 copy-start.51
  366.8 7.2 copy-start.4
  366.8 7.2 copy-start.9
  366.8 7.2 copy-start.54
  366.8 11.3 %slice-start = ((s8[4718592]{0:T(1024)(128)(4,1)}), s8[4194304]{0:T(1024)(128)(4,1)S(1)}, s32[]{:S(2)}) async-start(s8[4718592]{0:T(1024)(128)(4,1)} %bitcast.83), calls=%async_computation.18 | async-start | bytes 8388608
  373.9 6.4 copy-start.39
  374.0 4.1 copy-start.2
  374.0 4.1 slice-start.1
  378.1 3.8 copy-start.27
  383.9 203.2 %reduce-scatter.11.cloned.1.call-start = ((), (), s32[]{:S(2)}) async-start(), calls=%async_computation.14 | async-start | bytes 2433024 | tf_op jit(solution)/shard_map/reduce_scatter | solution.py:206
  394.4 297.1 %reduce-scatter.9.cloned.1.call-start = ((), (), s32[]{:S(2)}) async-start(), calls=%async_computation.13 | async-start | bytes 2433024 | tf_op jit(solution)/shard_map/reduce_scatter | solution.py:205
  401.8 394.0 %reduce-scatter.7.cloned.1.call-start = ((), (), s32[]{:S(2)}) async-start(), calls=%async_computation.12 | async-start | bytes 2433024 | tf_op jit(solution)/shard_map/reduce_scatter | solution.py:204
  405.0 532.8 %reduce-scatter.17.cloned.1.call-start = ((), (), s32[]{:S(2)}) async-start(), calls=%async_computation.17 | async-start | bytes 9732096 | tf_op jit(solution)/shard_map/reduce_scatter | solution.py:209
  412.1 667.3 %reduce-scatter.15.cloned.1.call-start = ((), (), s32[]{:S(2)}) async-start(), calls=%async_computation.16 | async-start | bytes 9732096 | tf_op jit(solution)/shard_map/reduce_scatter | solution.py:208
  418.9 4.6 copy-start.12
  418.9 4.6 copy-start.28
  418.9 5.1 copy-start.19
  420.1 3.9 copy-start.29
  423.5 43.7 %copy-start.40 = (f32[256]{0:T(256)S(1)}, f32[256]{0:T(256)}, u32[]{:S(2)}) copy-start(f32[256]{0:T(256)} %copy-done.39) | copy-start | bytes 3076
  424.1 49.5 %copy-start.44 = (f32[256]{0:T(256)S(1)}, f32[256]{0:T(256)}, u32[]{:S(2)}) copy-start(f32[256]{0:T(256)} %copy-done.43) | copy-start | bytes 3076
  424.1 49.5 %copy-start.10 = (bf16[256,768]{1,0:T(8,128)(2,1)S(1)}, bf16[256,768]{1,0:T(8,128)(2,1)}, u32[]{:S(2)}) copy-start(bf16[256,768]{1,0:T(8,128)(2,1)} %gather_fusion.2) | copy-start | bytes 1179652
  424.1 49.5 %copy-start.22 = (f32[256,768]{1,0:T(8,128)S(1)}, f32[256,768]{1,0:T(8,128)}, u32[]{:S(2)}) copy-start(f32[256,768]{1,0:T(8,128)} %copy-done.21) | copy-start | bytes 2359300
  424.1 49.5 %copy-start.35 = (f32[256]{0:T(256)S(1)}, f32[256]{0:T(256)}, u32[]{:S(2)}) copy-start(f32[256]{0:T(256)} %copy-done.34) | copy-start | bytes 3076
  424.1 49.5 %copy-start.42 = (f32[768]{0:T(1024)S(1)}, f32[768]{0:T(1024)}, u32[]{:S(2)}) copy-start(f32[768]{0:T(1024)} %convert_element_type.179) | copy-start | bytes 9220
  424.1 49.5 %copy-start.46 = (f32[256]{0:T(256)S(1)}, f32[256]{0:T(256)}, u32[]{:S(2)}) copy-start(f32[256]{0:T(256)} %copy-done.45) | copy-start | bytes 3076
  424.1 49.5 %copy-start.53 = (f32[256]{0:T(256)S(1)}, f32[256]{0:T(256)}, u32[]{:S(2)}) copy-start(f32[256]{0:T(256)} %get-tuple-element.21) | copy-start | bytes 3076
  425.7 47.9 %copy-start.23 = (f32[256,768]{1,0:T(8,128)S(1)}, f32[256,768]{1,0:T(8,128)}, u32[]{:S(2)}) copy-start(f32[256,768]{1,0:T(8,128)} %get-tuple-element.36) | copy-start | bytes 2359300
  425.7 48.0 %copy-start.37 = (f32[256]{0:T(256)S(1)}, f32[256]{0:T(256)}, u32[]{:S(2)}) copy-start(f32[256]{0:T(256)} %copy-done.36) | copy-start | bytes 3076
  473.6 605.8 %copy-start.1 = (s32[1,2048]{1,0:T(1,128)S(1)}, s32[1,2048]{1,0:T(1,128)}, u32[]{:S(2)}) copy-start(s32[1,2048]{1,0:T(1,128)} %param.16) | copy-start | bytes 24580
  (24 other events, 35.9 us)
Sparse Core Ops, SparseCore 0:
  11.6 56.8 all-gather.8
  71.5 53.0 all-gather.10
  127.6 52.9 all-gather.6
  183.5 52.9 all-gather.12
  239.4 62.4 all-gather.14
  304.8 61.9 all-gather.16
  384.0 98.4 reduce-scatter.12
  488.4 98.5 reduce-scatter.10
  592.9 98.5 reduce-scatter.8
  697.2 98.5 reduce-scatter.6
  802.3 135.5 reduce-scatter.16
  944.2 135.1 reduce-scatter.14
where the time goes:
time: 1090 us
  waiting for transfers between devices  876 us (80%)
  blocking collectives  81.8 us (8%)
  matrix products  63.9 us (6%)
  local copies, waits for them, and re-layouts  28.3 us (3%)
  other arithmetic  20.9 us (2%)
  between operations  14.9 us (1%)
    reduce_scatter x1, waiting for transfers between devices, body(): lax.psum_scatter(grad_shrink, ('gx', 'gy'), scatter_dimension=0, tiled=True)  142 us
    reduce_scatter x1, waiting for transfers between devices, body(): lax.psum_scatter(grad_expand, ('gx', 'gy'), scatter_dimension=0, tiled=True)  142 us
    reduce_scatter x1, waiting for transfers between devices, body(): lax.psum_scatter(grad_value, ('gx', 'gy'), scatter_dimension=0, tiled=True)  104 us
    reduce_scatter x1, waiting for transfers between devices, body(): lax.psum_scatter(grad_key, ('gx', 'gy'), scatter_dimension=0, tiled=True)  104 us
    reduce_scatter x1, waiting for transfers between devices, body(): lax.psum_scatter(grad_query, ('gx', 'gy'), scatter_dimension=0, tiled=True)  104 us
    unnamed x2, blocking collectives  81.8 us
    all_gather x1, waiting for transfers between devices, body(): lax.all_gather(expand_weight, ('gx', 'gy'), axis=0, tiled=True)  61.8 us
    all_gather x1, waiting for transfers between devices, body(): lax.all_gather(shrink_weight, ('gx', 'gy'), axis=0, tiled=True)  59.1 us
  transfers between devices with their start and end apart: 12, of which 11 were waited for; matrix products, arithmetic and copies ran while one was open for 8% of the time, Pallas kernels for 0%

commit v1 on v0

v1 whole, which is shorter than its diff:
```python
from functools import partial

import jax
import jax.numpy as jnp
from jax import lax
from jax.experimental import pallas as pl
from jax.experimental.pallas import tpu as pltpu
from jax.sharding import PartitionSpec as P

HEAD_DIM = 64


SCALE = 0.125
EPS = 1e-06
NEGATIVE = -1e30


def rms_norm(values, gain):
    return values * lax.rsqrt(jnp.mean(values * values, axis=-1, keepdims=True) + EPS) * gain


def matmul(left, right):
    return jnp.dot(left, right, preferred_element_type=jnp.float32)


def matmul_left_t(left, right):
    return lax.dot_general(
        left, right, (((0,), (0,)), ((), ())), preferred_element_type=jnp.float32
    )


def matmul_right_t(left, right):
    return lax.dot_general(
        left, right, (((1,), (1,)), ((), ())), preferred_element_type=jnp.float32
    )


GX, GY = "gx", "gy"
BOTH = (GX, GY)
LANES = 128
ATTN_ORDER = ("21yx", "12xy")
EXPAND_ORDER = ("1x2y", "2y1x")
SHRINK_ORDER = ("yx21", "y21x")


def log2(size):
    return size.bit_length() - 1


def stage_masks(sizes, order):
    low = log2(sizes[GY])
    letters = {
        "x": [low] if sizes[GX] > 1 else [],
        "y": [low + bit for bit in reversed(range(1, log2(sizes[GX])))],
        "1": [1] if low > 1 else [],
        "2": list(reversed(range(2, low))),
    }
    return tuple(tuple(bit for letter in way for bit in letters[letter]) for way in order)


def exchange(value, sizes, bits):
    count = sizes[GX] * sizes[GY]
    pairs = [(i, i ^ (1 << bits[i & 1])) for i in range(count)]
    return lax.ppermute(value, BOTH, pairs)


def by_core(first, second):
    zero = lax.axis_index(BOTH) % 2 == 0
    return jnp.where(zero, first, second), jnp.where(zero, second, first)


def gather(halves, sizes, ways):
    mine, other = by_core(*halves)
    arrived = exchange(other, sizes, (0, 0))
    current = jnp.stack(by_core(mine, arrived))[None]
    for bits in zip(*ways):
        current = jnp.concatenate([current, exchange(current, sizes, bits)], 0)
    return current, exchange(current, sizes, (0, 0))


def scatter_sum(mine, other, sizes, ways):
    current = mine.astype(jnp.float32) + exchange(other, sizes, (0, 0)).astype(jnp.float32)
    for bits in reversed(list(zip(*ways))):
        count = current.shape[0] // 2
        arrived = exchange(current[count:].astype(jnp.bfloat16), sizes, bits)
        current = current[:count] + arrived.astype(jnp.float32)
    kept, sent = by_core(current[0, 0], current[0, 1])
    return by_core(kept, exchange(sent.astype(jnp.bfloat16), sizes, (0, 0)).astype(jnp.float32))


def slot(chip, own, way):
    apart = chip ^ own
    total = 0
    for stage, bit in enumerate(way):
        total = total + (((apart >> (bit - 1)) & 1) << stage)
    return total


def chip_slots(count, way):
    return slot(jnp.arange(count), lax.axis_index(BOTH) // 2, way)


class Piece:
    def __init__(self, shapes, rows, step, offsets, columns):
        self.shapes, self.rows, self.step, self.offsets, self.columns = (
            shapes,
            rows,
            step,
            offsets,
            columns,
        )


def assemble(own, arrived, piece, ways):
    chips, _, rows, width = own.shape
    if rows % 8:
        first, second = by_core(own, arrived)
        outs = [jnp.zeros((chips, 2, piece.step, s[1]), jnp.bfloat16) for s in piece.shapes]
        for half, array in enumerate((first, second)):
            array = jnp.take(array, chip_slots(chips, ways[half]), axis=0)
            top = piece.offsets[half]
            for out, source, target, size in piece.columns[half]:
                outs[out] = (
                    outs[out]
                    .at[:, :, top : top + rows, target : target + size]
                    .set(array[:, :, :, source : source + size])
                )
        return [out.reshape(shape) for out, shape in zip(outs, piece.shapes)]
    joined = piece.step == rows
    height = 2 * rows if joined else rows

    def kernel(place, own_ref, arrived_ref, *rest):
        outs, sems = rest[: len(piece.shapes)], rest[len(piece.shapes)]
        core, chip = place[0], place[1]

        def copies(sources):
            def one(q, carry):
                for half in range(2):
                    at = slot(q, chip, ways[half])
                    for j in range(1 if joined else 2):
                        block = sources[half].at[at if joined else 2 * at + j]
                        top = (2 * q + j) * piece.step + piece.offsets[half]
                        top = pl.multiple_of(top, 8)
                        for out, source, target, size in piece.columns[half]:
                            pltpu.make_async_copy(
                                block.at[:, pl.ds(source, size)],
                                outs[out].at[pl.ds(top, height), pl.ds(target, size)],
                                sems.at[out],
                            ).start()
                return carry

            lax.fori_loop(0, chips, one, 0)

        @pl.when(core == 0)
        def _():
            copies((own_ref, arrived_ref))

        @pl.when(core == 1)
        def _():
            copies((arrived_ref, own_ref))

        for out, ref in enumerate(outs):
            pltpu.make_async_copy(ref, ref, sems.at[out]).wait()

    flat = (chips, height, width) if joined else (2 * chips, height, width)
    device = lax.axis_index(BOTH)
    place = jnp.stack([device % 2, device // 2]).astype(jnp.int32)
    total = sum(s[0] * s[1] for s in piece.shapes)
    return pl.pallas_call(
        kernel,
        out_shape=[jax.ShapeDtypeStruct(s, jnp.bfloat16) for s in piece.shapes],
        in_specs=[
            pl.BlockSpec(memory_space=pltpu.SMEM),
            pl.BlockSpec(memory_space=pl.ANY),
            pl.BlockSpec(memory_space=pl.ANY),
        ],
        out_specs=[pl.BlockSpec(memory_space=pltpu.VMEM) for _ in piece.shapes],
        scratch_shapes=[pltpu.SemaphoreType.DMA((len(piece.shapes),))],
        compiler_params=pltpu.CompilerParams(vmem_limit_bytes=24 << 20),
        cost_estimate=pl.CostEstimate(flops=0, bytes_accessed=4 * total, transcendentals=0),
        name="assemble",
    )(place, own.reshape(flat), arrived.reshape(flat))


def spread(products, extra, piece, ways, chips, width):
    rows = piece.rows
    count = len(piece.shapes)

    def product(left, right):
        return lax.dot_general(
            left, right, (((0,), (0,)), ((), ())), preferred_element_type=jnp.float32
        )

    if rows % 8:
        full = [
            (product(*products[i]) if i in products else extra).astype(jnp.bfloat16)
            for i in range(count)
        ]
        halves = []
        for half in range(2):
            array = jnp.zeros((chips, 2, rows, width), jnp.bfloat16)
            top = piece.offsets[half]
            for out, source, target, size in piece.columns[half]:
                part = full[out].reshape(chips, 2, piece.step, -1)
                array = array.at[:, :, :, source : source + size].set(
                    part[:, :, top : top + rows, target : target + size]
                )
            index = jnp.zeros((chips,), jnp.int32).at[chip_slots(chips, ways[half])].set(
                jnp.arange(chips, dtype=jnp.int32)
            )
            halves.append(jnp.take(array, index, axis=0))
        return by_core(*halves)
    joined = piece.step == rows
    height = 2 * rows if joined else rows
    lefts, rights, uses = [], [], {}
    for i, (left, right) in products.items():
        for group, value in ((lefts, left), (rights, right)):
            if not any(value is v for v in group):
                group.append(value)
        uses[i] = (
            [left is v for v in lefts].index(True),
            [right is v for v in rights].index(True),
        )
    operands = lefts + rights + ([extra] if extra is not None else [])

    def kernel(place, *refs):
        left_refs, right_refs = refs[: len(lefts)], refs[len(lefts) : len(lefts) + len(rights)]
        rest = refs[len(lefts) + len(rights) :]
        if extra is not None:
            extra_ref, rest = rest[0], rest[1:]
        mine, other = rest[0], rest[1]
        held = dict(zip(uses, rest[2:]))
        sems = rest[2 + len(uses)]
        core, chip = place[0], place[1]

        def copies(out):
            source_ref = held[out] if out in held else extra_ref

            def send(targets):
                def one(q, carry):
                    for half in range(2):
                        at = slot(q, chip, ways[half])
                        for j in range(1 if joined else 2):
                            block = targets[half].at[at if joined else 2 * at + j]
                            top = (2 * q + j) * piece.step + piece.offsets[half]
                            top = pl.multiple_of(top, 8)
                            for index, source, target, size in piece.columns[half]:
                                if index == out:
                                    pltpu.make_async_copy(
                                        source_ref.at[pl.ds(top, height), pl.ds(target, size)],
                                        block.at[:, pl.ds(source, size)],
                                        sems.at[out],
                                    ).start()
                    return carry

                lax.fori_loop(0, chips, one, 0)

            @pl.when(core == 0)
            def _():
                send((mine, other))

            @pl.when(core == 1)
            def _():
                send((other, mine))

        if extra is not None:
            copies(count - 1)
        for out, (l, r) in uses.items():
            deep, wide = piece.shapes[out]
            tile = 256
            left_ref, right_ref, target_ref = left_refs[l], right_refs[r], held[out]

            def step(i, carry, left_ref=left_ref, right_ref=right_ref, target_ref=target_ref):
                at = pl.multiple_of(i * tile, tile)
                target_ref[pl.ds(at, tile), :] = product(
                    left_ref[:, pl.ds(at, tile)], right_ref[...]
                ).astype(jnp.bfloat16)
                return carry

            lax.fori_loop(0, deep // tile, step, 0)
            copies(out)
        for out in range(count):
            ref = held[out] if out in held else extra_ref
            times = sum(1 for half in range(2) for c in piece.columns[half] if c[0] == out)
            full_columns = sum(c[3] for half in range(2) for c in piece.columns[half] if c[0] == out)
            repeat = full_columns // piece.shapes[out][1] if joined else 1
            for _ in range(max(repeat, 1)):
                pltpu.make_async_copy(ref, ref, sems.at[out]).wait()

    flat = (chips, height, width) if joined else (2 * chips, height, width)
    device = lax.axis_index(BOTH)
    place = jnp.stack([device % 2, device // 2]).astype(jnp.int32)
    total = sum(s[0] * s[1] for s in piece.shapes)
    mine, other = pl.pallas_call(
        kernel,
        out_shape=[jax.ShapeDtypeStruct(flat, jnp.bfloat16)] * 2,
        in_specs=[pl.BlockSpec(memory_space=pltpu.SMEM)]
        + [pl.BlockSpec(memory_space=pltpu.VMEM) for _ in operands],
        out_specs=[pl.BlockSpec(memory_space=pl.ANY)] * 2,
        scratch_shapes=[pltpu.VMEM(piece.shapes[i], jnp.bfloat16) for i in uses]
        + [pltpu.SemaphoreType.DMA((count,))],
        compiler_params=pltpu.CompilerParams(vmem_limit_bytes=40 << 20),
        cost_estimate=pl.CostEstimate(
            flops=512 * total, bytes_accessed=2 * total, transcendentals=0
        ),
        name="spread",
    )(place, *operands)
    shape = (chips, 2, rows, width)
    return mine.reshape(shape), other.reshape(shape)


def body(
    sizes,
    tokens,
    cotangent,
    chosen,
    segment,
    router,
    gain_one,
    gain_two,
    query_weight,
    key_weight,
    value_weight,
    output_weight,
    expand_weight,
    shrink_weight,
):
    row_count, seq_len, width = tokens.shape
    keep_count = chosen.shape[1]
    hidden_units = expand_weight.shape[1]
    chips = sizes[GX] * sizes[GY] // 2
    attn_ways = stage_masks(sizes, ATTN_ORDER)
    expand_ways = stage_masks(sizes, EXPAND_ORDER)
    shrink_ways = stage_masks(sizes, SHRINK_ORDER)
    rows = query_weight.shape[0]
    half_units = hidden_units // 2
    attn_width = 2 * width + LANES
    attn_piece = Piece(
        [(width, width)] * 4 + [(width, LANES)],
        rows,
        rows,
        (0, 0),
        (
            ((0, 0, 0, width), (1, width, 0, width), (4, 2 * width, 0, LANES)),
            ((2, 0, 0, width), (3, width, 0, width)),
        ),
    )
    expand_piece = Piece(
        [(width, hidden_units)],
        rows,
        rows,
        (0, 0),
        (((0, 0, 0, half_units),), ((0, 0, half_units, half_units),)),
    )
    half_rows = shrink_weight.shape[0] // 2
    shrink_piece = Piece(
        [(hidden_units, width)],
        half_rows,
        2 * half_rows,
        (0, half_rows),
        (((0, 0, 0, width),), ((0, 0, 0, width),)),
    )
    small = jnp.stack([router, gain_one, gain_two], axis=1)
    small = jnp.pad(small, ((0, 0), (0, LANES - small.shape[1])))
    attn_halves = (
        jnp.concatenate([query_weight, key_weight, small], axis=1),
        jnp.concatenate([value_weight, output_weight, small], axis=1),
    )
    attn_pair = gather(attn_halves, sizes, attn_ways)
    expand_pair = gather(
        (expand_weight[:, :half_units], expand_weight[:, half_units:]), sizes, expand_ways
    )
    shrink_pair = gather((shrink_weight[:half_rows], shrink_weight[half_rows:]), sizes, shrink_ways)
    query_all, key_all, value_all, output_all, small_all = assemble(
        *attn_pair, attn_piece, attn_ways
    )
    (expand_all,) = assemble(*expand_pair, expand_piece, expand_ways)
    (shrink_all,) = assemble(*shrink_pair, shrink_piece, shrink_ways)
    router_all, gain_one_all, gain_two_all = [small_all[:, i] for i in range(3)]
    head_size = HEAD_DIM
    head_count = width // head_size
    token_count = row_count * keep_count
    picked = chosen[:, :, None] == jnp.arange(seq_len, dtype=chosen.dtype)
    one_hot = picked.astype(jnp.bfloat16)
    hit = jnp.any(picked, axis=1)[:, :, None]

    def take_rows(array):
        taken = jnp.einsum("rks,rsd->rkd", one_hot, array, preferred_element_type=jnp.float32)
        return taken.astype(jnp.bfloat16).reshape(token_count, width)

    def put_rows(array, values):
        values = values.astype(jnp.bfloat16).reshape(row_count, keep_count, width)
        placed = jnp.einsum("rks,rkd->rsd", one_hot, values, preferred_element_type=jnp.float32)
        return jnp.where(hit, placed.astype(jnp.bfloat16), array)

    hidden_low = take_rows(tokens)
    hidden = hidden_low.astype(jnp.float32)
    router_gate = jax.nn.sigmoid(matmul(hidden_low, router_all))
    normed = rms_norm(hidden, gain_one_all.astype(jnp.float32)).astype(jnp.bfloat16)
    head_shape = (row_count, keep_count, head_count, head_size)
    queries = matmul(normed, query_all).astype(jnp.bfloat16).reshape(head_shape)
    key_rows = matmul(normed, key_all).astype(jnp.bfloat16).reshape(head_shape)
    value_rows = matmul(normed, value_all).astype(jnp.bfloat16).reshape(head_shape)
    labels = jnp.sum(jnp.where(picked, segment[:, None, :], 0), axis=-1)
    allowed = (
        (chosen[:, None, :] <= chosen[:, :, None]) & (labels[:, None, :] == labels[:, :, None])
    )[:, None]

    def attn_scores():
        raw_scores = (
            jnp.einsum("rqhd,rkhd->rhqk", queries, key_rows, preferred_element_type=jnp.float32)
            * SCALE
        )
        return jnp.where(allowed, raw_scores, NEGATIVE)

    scores = attn_scores()
    peak = jnp.max(scores, axis=-1, keepdims=True)
    exp_terms = jnp.exp(scores - peak)
    total_mass = jnp.sum(exp_terms, axis=-1, keepdims=True)
    probs_low = (exp_terms / total_mass).astype(jnp.bfloat16)
    log_mass = peak + jnp.log(total_mass)
    attn_mixed = (
        jnp.einsum("rhqk,rkhd->rqhd", probs_low, value_rows, preferred_element_type=jnp.float32)
        .astype(jnp.bfloat16)
        .reshape(token_count, width)
    )
    attn_out = matmul(attn_mixed, output_all)
    middle = hidden + attn_out
    normed_two = rms_norm(middle, gain_two_all.astype(jnp.float32)).astype(jnp.bfloat16)
    pre_act = matmul(normed_two, expand_all)
    gelu_values, gelu_back = jax.vjp(partial(jax.nn.gelu, approximate=True), pre_act)
    activated = gelu_values.astype(jnp.bfloat16)
    mlp_out = matmul(activated, shrink_all)
    branch = attn_out + mlp_out
    updated = hidden + router_gate[:, None] * branch
    out_tokens = put_rows(tokens, updated)
    router_back, gain_one_back, gain_two_back = router_all, gain_one_all, gain_two_all
    query_back, key_back, value_back, output_back = query_all, key_all, value_all, output_all
    expand_back, shrink_back = expand_all, shrink_all
    cot_rows = take_rows(cotangent).astype(jnp.float32)
    grad_branch = router_gate[:, None] * cot_rows
    logit_low = (jnp.sum(cot_rows * branch, axis=-1) * router_gate * (1.0 - router_gate)).astype(
        jnp.bfloat16
    )
    grad_router = matmul(logit_low, hidden_low)
    mlp_low = grad_branch.astype(jnp.bfloat16)
    shrink_parts = scatter_sum(
        *spread({0: (activated, mlp_low)}, None, shrink_piece, shrink_ways, chips, width),
        sizes,
        shrink_ways,
    )
    (grad_pre,) = gelu_back(matmul_right_t(mlp_low, shrink_back))
    pre_low = grad_pre.astype(jnp.bfloat16)
    expand_parts = scatter_sum(
        *spread({0: (normed_two, pre_low)}, None, expand_piece, expand_ways, chips, half_units),
        sizes,
        expand_ways,
    )
    grad_normed_two = matmul_right_t(pre_low, expand_back)
    norm_two_value, norm_two_back = jax.vjp(rms_norm, middle, gain_two_back.astype(jnp.float32))
    grad_middle, grad_gain_two = norm_two_back(grad_normed_two)
    attn_low = (grad_middle + grad_branch).astype(jnp.bfloat16)
    mixed_low = matmul_right_t(attn_low, output_back).astype(jnp.bfloat16).reshape(head_shape)
    probs_again = jnp.exp(attn_scores() - log_mass)
    probs_again_low = probs_again.astype(jnp.bfloat16)
    dvalue_low = (
        jnp.einsum(
            "rhqk,rqhd->rkhd", probs_again_low, mixed_low, preferred_element_type=jnp.float32
        )
        .astype(jnp.bfloat16)
        .reshape(token_count, width)
    )
    grad_probs = jnp.einsum(
        "rqhd,rkhd->rhqk", mixed_low, value_rows, preferred_element_type=jnp.float32
    )
    scores_low = (
        probs_again * (grad_probs - jnp.sum(probs_again * grad_probs, axis=-1, keepdims=True))
    ).astype(jnp.bfloat16)
    dquery_low = (
        (
            jnp.einsum("rhqk,rkhd->rqhd", scores_low, key_rows, preferred_element_type=jnp.float32)
            * SCALE
        )
        .astype(jnp.bfloat16)
        .reshape(token_count, width)
    )
    dkey_low = (
        (
            jnp.einsum("rhqk,rqhd->rkhd", scores_low, queries, preferred_element_type=jnp.float32)
            * SCALE
        )
        .astype(jnp.bfloat16)
        .reshape(token_count, width)
    )
    grad_normed = (
        matmul_right_t(dquery_low, query_back)
        + matmul_right_t(dkey_low, key_back)
        + matmul_right_t(dvalue_low, value_back)
    )
    norm_one_value, norm_one_back = jax.vjp(rms_norm, hidden, gain_one_back.astype(jnp.float32))
    norm_back, grad_gain_one = norm_one_back(grad_normed)
    grad_hidden = (
        cot_rows
        + grad_middle
        + norm_back
        + logit_low.astype(jnp.float32)[:, None] * router_back.astype(jnp.float32)[None, :]
    )
    grad_tokens = put_rows(cotangent, grad_hidden)
    grad_small = jnp.stack([grad_router, grad_gain_one, grad_gain_two], axis=1)
    grad_small = jnp.pad(grad_small, ((0, 0), (0, LANES - grad_small.shape[1])))
    attn_parts = scatter_sum(
        *spread(
            {
                0: (normed, dquery_low),
                1: (normed, dkey_low),
                2: (normed, dvalue_low),
                3: (attn_mixed, attn_low),
            },
            grad_small.astype(jnp.bfloat16),
            attn_piece,
            attn_ways,
            chips,
            attn_width,
        ),
        sizes,
        attn_ways,
    )
    shares = (
        attn_parts[0][:, 2 * width],
        attn_parts[0][:, 2 * width + 1],
        attn_parts[0][:, 2 * width + 2],
        attn_parts[0][:, :width],
        attn_parts[0][:, width : 2 * width],
        attn_parts[1][:, :width],
        attn_parts[1][:, width : 2 * width],
        jnp.concatenate(expand_parts, axis=1),
        jnp.concatenate(shrink_parts, axis=0),
    )
    return (
        out_tokens,
        grad_tokens,
        shares[0],
        shares[1],
        shares[2],
        shares[3],
        shares[4],
        shares[5],
        shares[6],
        shares[7],
        shares[8],
    )


def solution(mesh):
    in_specs = (
        P(("gx", "gy"), None, None),
        P(("gx", "gy"), None, None),
        P(("gx", "gy"), None),
        P(("gx", "gy"), None),
        P(("gx", "gy")),
        P(("gx", "gy")),
        P(("gx", "gy")),
        P(("gx", "gy"), None),
        P(("gx", "gy"), None),
        P(("gx", "gy"), None),
        P(("gx", "gy"), None),
        P(("gx", "gy"), None),
        P(("gx", "gy"), None),
    )
    out_specs = (
        P(("gx", "gy"), None, None),
        P(("gx", "gy"), None, None),
        P(("gx", "gy")),
        P(("gx", "gy")),
        P(("gx", "gy")),
        P(("gx", "gy"), None),
        P(("gx", "gy"), None),
        P(("gx", "gy"), None),
        P(("gx", "gy"), None),
        P(("gx", "gy"), None),
        P(("gx", "gy"), None),
    )
    return jax.shard_map(partial(body, dict(mesh.shape)), mesh=mesh, in_specs=in_specs, out_specs=out_specs, check_vma=False)
```

time: 1090 us -> 293 us (0.27)
  waiting for transfers between devices: 876 us -> 98.6 us
  blocking collectives: 81.8 us -> 0 us
  starting transfers between devices: 0.7 us -> 64.2 us
  Pallas kernels: 0 us -> 29.2 us
  matrix products: 63.9 us -> 41.3 us
  between operations: 14.9 us -> 2.1 us
    reduce_scatter x6 -> x0, waiting for transfers between devices: 599 us -> none  [the longest x1 142 us: body(): lax.psum_scatter(grad_shrink, ('gx', 'gy'), scatter_dimension=0, tiled=True)]
    all_gather x6 -> x0, waiting for transfers between devices: 273 us -> none  [the longest x1 61.8 us: body(): lax.all_gather(expand_weight, ('gx', 'gy'), axis=0, tiled=True)]
    ppermute x0 -> x36, waiting for transfers between devices: none -> 98.6 us  [exchange(): return lax.ppermute(value, BOTH, pairs)]
    unnamed x2 -> x0, blocking collectives: 81.8 us -> none
    ppermute x0 -> x36, starting transfers between devices: none -> 64.2 us  [exchange(): return lax.ppermute(value, BOTH, pairs)]
    pallas_call x0 -> x6, Pallas kernels: none -> 29.2 us  [the longest x3 18.4 us: spread(): pl.pallas_call(kernel, out_shape=[jax.ShapeDtypeStruct(flat, jnp.bfloat16...]
    scatter x2 -> x0, other arithmetic: 12.6 us -> none  [the longest x1 6.37 us: body(): tokens.at[row_ids, chosen]]
    dot_general x8, matrix products: 23.1 us -> 12 us  [matmul(): return jnp.dot(left, right, preferred_element_type=jnp.float32)]
  transfers between devices with their start and end apart: 12 -> 36, of which waited for: 11 -> 14; matrix products, arithmetic and copies ran while one was open for 8% -> 15% of each run, Pallas kernels for 0% -> 8%
where the time goes in v1:
time: 293 us; the launch traced here: 292 us
  waiting for transfers between devices  98.6 us (34%)
  starting transfers between devices  64.2 us (22%)
  matrix products  41.3 us (14%)
  local copies, waits for them, and re-layouts  35.5 us (12%)
  Pallas kernels  29.2 us (10%)
  other arithmetic  21.4 us (7%)
    ppermute x36, waiting for transfers between devices, exchange(): return lax.ppermute(value, BOTH, pairs)  98.6 us
    ppermute x36, starting transfers between devices, exchange(): return lax.ppermute(value, BOTH, pairs)  64.2 us
    pallas_call x3, Pallas kernels, spread(): pl.pallas_call(kernel, out_shape=[jax.ShapeDtypeStruct(flat, jnp.bfloat16...  18.4 us
    unnamed x160, local copies, waits for them, and re-layouts  14.8 us
    dot_general x8, matrix products, matmul(): return jnp.dot(left, right, preferred_element_type=jnp.float32)  12 us
    pallas_call x3, Pallas kernels, assemble(): pl.pallas_call(kernel, out_shape=[jax.ShapeDtypeStruct(s, jnp.bfloat16) f...  10.8 us
    dot_general x6, matrix products, matmul_right_t(): lax.dot_general(left, right, (((1,), (1,)), ((), ())), preferred_element_...  9.65 us
    dot_general x2, matrix products, put_rows(): jnp.einsum('rks,rkd->rsd', one_hot, values, preferred_element_type=jnp.fl...  8.53 us
  transfers between devices with their start and end apart: 36, of which 14 were waited for; matrix products, arithmetic and copies ran while one was open for 15% of the time, Pallas kernels for 8%

profile of v1, /device:TPU:0, one launch (start us, length us, event | category | flops | bytes accessed | tf_op | source)
XLA Modules:
  0.0 292.2 jit_solution(15113248031785109018)
XLA Ops:
  8.0 3.1 %fusion.54 = (f32[256]{0:T(256)S(1)}, bf16[256,768]{1,0:T(8,128)(2,1)S(1)}) fusion(bf16[1,2048,768]{2,1,0:T(8,128)(2,1)} %param.13, s32[256]{0:T(256)} %bitcast.208), kind=kOutput, calls=%fused_computation.89 | convolution fusion | flops 806616832 | bytes 3540992 | tf_op jit(solution)/shard_map/rks,rsd->rkd/dot_general | solution.py:388
  11.9 2.6 collective-permute-start.13
  16.2 2.7 collective-permute-start.1
  18.9 4.9 %collective-permute-done.7 = bf16[1,2,24,1536]{3,2,1,0:T(8,128)(2,1)S(1)} collective-permute-done((bf16[1,2,24,1536]{3,2,1,0:T(8,128)(2,1)S(1)}, bf16[1,2,24,1536]{3,2,1,0:T(8,128)(2,1)S(1)}, u32[]{:S(2)}, u32[]{:S(2)}) %collective-permute-start.7) | collective-permute-done | bytes 147488 | tf_op jit(solution)/shard_map/ppermute | solution.py:64
  26.5 7.3 %collective-permute-done.14 = bf16[2,2,48,768]{3,2,1,0:T(8,128)(2,1)S(1)} collective-permute-done((bf16[2,2,48,768]{3,2,1,0:T(8,128)(2,1)S(1)}, bf16[2,2,48,768]{3,2,1,0:T(8,128)(2,1)S(1)}, u32[]{:S(2)}, u32[]{:S(2)}) %collective-permute-start.14) | collective-permute-done | bytes 294944 | tf_op jit(solution)/shard_map/ppermute | solution.py:64
  36.2 2.6 collective-permute-start.9
  38.8 13.5 %collective-permute-done.15 = bf16[4,2,48,768]{3,2,1,0:T(8,128)(2,1)S(1)} collective-permute-done((bf16[4,2,48,768]{3,2,1,0:T(8,128)(2,1)S(1)}, bf16[4,2,48,768]{3,2,1,0:T(8,128)(2,1)S(1)}, u32[]{:S(2)}, u32[]{:S(2)}) %collective-permute-start.15) | collective-permute-done | bytes 589856 | tf_op jit(solution)/shard_map/ppermute | solution.py:64
  55.7 8.6 %collective-permute-done.9 = bf16[4,2,24,1536]{3,2,1,0:T(8,128)(2,1)S(1)} collective-permute-done((bf16[4,2,24,1536]{3,2,1,0:T(8,128)(2,1)S(1)}, bf16[4,2,24,1536]{3,2,1,0:T(8,128)(2,1)S(1)}, u32[]{:S(2)}, u32[]{:S(2)}) %collective-permute-start.9) | collective-permute-done | bytes 589856 | tf_op jit(solution)/shard_map/ppermute | solution.py:64
  66.2 8.9 %collective-permute-done.16 = bf16[8,2,48,768]{3,2,1,0:T(8,128)(2,1)S(1)} collective-permute-done((bf16[8,2,48,768]{3,2,1,0:T(8,128)(2,1)S(1)}, bf16[8,2,48,768]{3,2,1,0:T(8,128)(2,1)S(1)}, u32[]{:S(2)}, u32[]{:S(2)}) %collective-permute-start.16) | collective-permute-done | bytes 1179680 | tf_op jit(solution)/shard_map/ppermute | solution.py:64
  75.3 9.9 %collective-permute-done.4 = bf16[8,2,24,1664]{3,2,1,0:T(8,128)(2,1)S(1)} collective-permute-done((bf16[8,2,24,1664]{3,2,1,0:T(8,128)(2,1)S(1)}, bf16[8,2,24,1664]{3,2,1,0:T(8,128)(2,1)S(1)}, u32[]{:S(2)}, u32[]{:S(2)}) %collective-permute-start.4) | collective-permute-done | bytes 1277984 | tf_op jit(solution)/shard_map/ppermute | solution.py:64
  85.5 4.3 %collective-permute-start.11 = (bf16[16,2,24,1536]{3,2,1,0:T(8,128)(2,1)S(1)}, bf16[16,2,24,1536]{3,2,1,0:T(8,128)(2,1)S(1)}, u32[]{:S(2)}, u32[]{:S(2)}) collective-permute-start(bf16[16,2,24,1536]{3,2,1,0:T(8,128)(2,1)S(1)} %constant_dynamic-update-slice_fusion.13), channel_id=1, source_target_pairs={{0,1},{1,0},{2,3},{3,2},{4,5},{5,4},{6,7},{7,6},{8,9},{9,8},{10,11... | collective-permute-start | bytes 7077896 | tf_op jit(solution)/shard_map/ppermute | solution.py:64
  90.4 6.9 %assemble.5 = bf16[3072,768]{1,0:T(8,128)(2,1)S(1)} custom-call(s32[2]{0:T(128)S(1)} %pad_add_fusion.place, bf16[32,48,768]{2,1,0:T(8,128)(2,1)S(1)} %bitcast.172, bf16[32,48,768]{2,1,0:T(8,128)(2,1)S(1)} %bitcast.177), custom_call_target="tpu_custom_call" | custom-call | bytes 9437184 | tf_op jit(solution)/shard_map/assemble/pallas_call | solution.py:169
  97.3 2.2 copy-done
  101.3 2.2 copy-done.1
  103.5 2.1 assemble.3
  111.5 2.7 convolution_convert_fusion.4
  114.2 1.9 copy.77
  116.1 2.5 convolution_convert_fusion.5
  118.6 1.9 copy.76
  126.4 2.1 multiply_convert_fusion.1
  132.9 3.2 %fusion.6.refs_1_ = bf16[256,3072]{1,0:T(8,128)(2,1)S(1)} fusion(f32[256,3072]{1,0:T(8,128)S(1)} %get-tuple-element.72, bf16[256,768]{1,0:T(8,128)(2,1)S(1)} %multiply_convert_fusion.3.refs_1_, bf16[3072,768]{1,0:T(8,128)(2,1)S(1)} %bitcast.169), kind=kOutput, calls=%fused_computation.13 | convolution fusion | flops 1223688192 | bytes 9830400 | tf_op jit(solution)/shard_map/dot_general | solution.py:33
  136.1 2.1 multiply_reduce_fusion.1
  142.4 2.7 fusion.23
  146.9 3.8 %spread.4 = (bf16[16,48,1536]{2,1,0:T(8,128)(2,1)S(1)}, bf16[16,48,1536]{2,1,0:T(8,128)(2,1)}) custom-call(s32[2]{0:T(128)S(1)} %pad_add_fusion.place, bf16[256,768]{1,0:T(8,128)(2,1)S(1)} %copy-done.12, bf16[256,3072]{1,0:T(8,128)(2,1)S(1)} %copy-done.14), custom_call_target="tpu_custom_call" | custom-call | flops 1207959552 | bytes 4718592 | tf_op jit(solution)/shard_map/spread/pallas_call | solution.py:294
  153.9 8.3 %spread.5 = (bf16[32,48,768]{2,1,0:T(8,128)(2,1)S(1)}, bf16[32,48,768]{2,1,0:T(8,128)(2,1)}) custom-call(s32[2]{0:T(128)S(1)} %pad_add_fusion.place, bf16[256,3072]{1,0:T(8,128)(2,1)S(1)} %copy-done.16, bf16[256,768]{1,0:T(8,128)(2,1)S(1)} %multiply_convert_fusion.3.refs_1_), custom_call_target="tpu_custom_call" | custom-call | flops 1207959552 | bytes 4718592 | tf_op jit(solution)/shard_map/spread/pallas_call | solution.py:294
  163.0 2.1 fusion.50
  167.0 1.9 copy.88.refs_4_
  169.0 1.9 copy.86.refs_2_
  170.9 1.9 copy.87.refs_3_
  181.1 6.3 %spread.3 = (bf16[16,48,1664]{2,1,0:T(8,128)(2,1)S(1)}, bf16[16,48,1664]{2,1,0:T(8,128)(2,1)S(1)}) custom-call(s32[2]{0:T(128)S(1)} %pad_add_fusion.place, bf16[256,768]{1,0:T(8,128)(2,1)S(1)} %fusion.49.refs_0_, bf16[256,768]{1,0:T(8,128)(2,1)S(1)} %copy.85.refs_1_, bf16[256,768]{1,0:T(8,128)(2,1)S(1)} %copy-done.9, bf16[256,768]{1,0:T(8,128)(2,1)S(1)} %copy-done.10, ...), custom_call_target="tpu_custom_call" | custom-call | flops 1258291200 | bytes 4915200 | tf_op jit(solution)/shard_map/spread/pallas_call | solution.py:294
  188.2 5.5 %bitcast_select_fusion = bf16[1,2048,768]{2,1,0:T(8,128)(2,1)} fusion(bf16[1,2048,768]{2,1,0:T(8,128)(2,1)} %param.14, pred[2048]{0:T(1024)(128)(4,1)S(1)} %fusion.13, s32[256]{0:T(256)S(1)} %bitcast.211, bf16[256,768]{1,0:T(8,128)(2,1)S(1)} %copy-done.21, f32[256,768]{1,0:T(8,128)S(1)} %copy-done.31, f32[256,768]{1,0:T(8,128)S(1)} %copy-done.37, ...), kind=kOutput, calls=%fused_computation.14 | convolution fusion | flops 812318720 | bytes 9847808 | tf_op jit(solution)/shard_map/rks,rkd->rsd/dot_general | solution.py:393
  193.7 2.4 convert_add_fusion.2
  196.2 2.6 collective-permute-start.25
  198.8 2.3 convert_add_fusion.1
  201.3 5.6 %collective-permute-start.31 = (bf16[8,2,48,768]{3,2,1,0:T(8,128)(2,1)S(1)}, bf16[8,2,48,768]{3,2,1,0:T(8,128)(2,1)S(1)}, u32[]{:S(2)}, u32[]{:S(2)}) collective-permute-start(bf16[8,2,48,768]{3,2,1,0:T(8,128)(2,1)S(1)} %slice.328), channel_id=1, source_target_pairs={{0,2},{1,9},{2,0},{3,11},{4,6},{5,13},{6,4},{7,15},{8,10},{9,1},{1... | collective-permute-start | bytes 3538952 | tf_op jit(solution)/shard_map/ppermute | solution.py:64
  209.1 3.1 %bitcast_select_fusion.1 = bf16[1,2048,768]{2,1,0:T(8,128)(2,1)} fusion(bf16[1,2048,768]{2,1,0:T(8,128)(2,1)S(1)} %copy-done.64, pred[2048]{0:T(1024)(128)(4,1)S(1)} %fusion.13, s32[256]{0:T(256)S(1)} %bitcast.212, bf16[256,768]{1,0:T(8,128)(2,1)S(1)} %copy-done.21, f32[256,768]{1,0:T(8,128)S(1)} %copy-done.66, f32[256]{0:T(256)S(1)} %copy-done.49), kind=kOutput, calls=%fused_computation.17 | convolution fusion | flops 809762816 | bytes 7475200 | tf_op jit(solution)/shard_map/rks,rkd->rsd/dot_general | solution.py:393
  212.2 9.1 %collective-permute-done.25 = bf16[8,2,24,1536]{3,2,1,0:T(8,128)(2,1)S(1)} collective-permute-done((bf16[8,2,24,1536]{3,2,1,0:T(8,128)(2,1)S(1)}, bf16[8,2,24,1536]{3,2,1,0:T(8,128)(2,1)S(1)}, u32[]{:S(2)}, u32[]{:S(2)}) %collective-permute-start.25) | collective-permute-done | bytes 1179680 | tf_op jit(solution)/shard_map/ppermute | solution.py:64
  221.7 4.2 %collective-permute-start.26 = (bf16[4,2,24,1536]{3,2,1,0:T(8,128)(2,1)S(1)}, bf16[4,2,24,1536]{3,2,1,0:T(8,128)(2,1)S(1)}, u32[]{:S(2)}, u32[]{:S(2)}) collective-permute-start(bf16[4,2,24,1536]{3,2,1,0:T(8,128)(2,1)S(1)} %slice.332), channel_id=1, source_target_pairs={{0,4},{1,3},{2,6},{3,1},{4,0},{5,7},{6,2},{7,5},{8,12},{9,11},{10,... | collective-permute-start | bytes 1769480 | tf_op jit(solution)/shard_map/ppermute | solution.py:64
  227.5 10.6 %collective-permute-done.19 = bf16[8,2,24,1664]{3,2,1,0:T(8,128)(2,1)S(1)} collective-permute-done((bf16[8,2,24,1664]{3,2,1,0:T(8,128)(2,1)S(1)}, bf16[8,2,24,1664]{3,2,1,0:T(8,128)(2,1)S(1)}, u32[]{:S(2)}, u32[]{:S(2)}) %collective-permute-start.19) | collective-permute-done | bytes 1277984 | tf_op jit(solution)/shard_map/ppermute | solution.py:64
  239.0 7.5 %collective-permute-done.26 = bf16[4,2,24,1536]{3,2,1,0:T(8,128)(2,1)S(1)} collective-permute-done((bf16[4,2,24,1536]{3,2,1,0:T(8,128)(2,1)S(1)}, bf16[4,2,24,1536]{3,2,1,0:T(8,128)(2,1)S(1)}, u32[]{:S(2)}, u32[]{:S(2)}) %collective-permute-start.26) | collective-permute-done | bytes 589856 | tf_op jit(solution)/shard_map/ppermute | solution.py:64
  248.2 4.6 %collective-permute-done.32 = bf16[4,2,48,768]{3,2,1,0:T(8,128)(2,1)S(1)} collective-permute-done((bf16[4,2,48,768]{3,2,1,0:T(8,128)(2,1)S(1)}, bf16[4,2,48,768]{3,2,1,0:T(8,128)(2,1)S(1)}, u32[]{:S(2)}, u32[]{:S(2)}) %collective-permute-start.32) | collective-permute-done | bytes 589856 | tf_op jit(solution)/shard_map/ppermute | solution.py:64
  255.6 4.1 %collective-permute-done.33 = bf16[2,2,48,768]{3,2,1,0:T(8,128)(2,1)S(1)} collective-permute-done((bf16[2,2,48,768]{3,2,1,0:T(8,128)(2,1)S(1)}, bf16[2,2,48,768]{3,2,1,0:T(8,128)(2,1)S(1)}, u32[]{:S(2)}, u32[]{:S(2)}) %collective-permute-start.33) | collective-permute-done | bytes 294944 | tf_op jit(solution)/shard_map/ppermute | solution.py:64
  259.9 2.4 collective-permute-start.34
  262.5 2.9 collective-permute-start.21
  265.4 7.6 %collective-permute-start.29 = (bf16[24,1536]{1,0:T(8,128)(2,1)S(1)}, bf16[24,1536]{1,0:T(8,128)(2,1)S(1)}, u32[]{:S(2)}, u32[]{:S(2)}) collective-permute-start(bf16[24,1536]{1,0:T(8,128)(2,1)S(1)} %fusion.69), channel_id=1, source_target_pairs={{0,1},{1,0},{2,3},{3,2},{4,5},{5,4},{6,7},{7,6},{8,9},{9,8},{10,11... | collective-permute-start | bytes 221192 | tf_op jit(solution)/shard_map/ppermute | solution.py:64
  273.1 2.0 collective-permute-start.35
  277.6 8.2 %collective-permute-done.22 = bf16[1,2,24,1664]{3,2,1,0:T(8,128)(2,1)S(1)} collective-permute-done((bf16[1,2,24,1664]{3,2,1,0:T(8,128)(2,1)S(1)}, bf16[1,2,24,1664]{3,2,1,0:T(8,128)(2,1)S(1)}, u32[]{:S(2)}, u32[]{:S(2)}) %collective-permute-start.22) | collective-permute-done | bytes 159776 | tf_op jit(solution)/shard_map/ppermute | solution.py:64
  285.9 3.8 %collective-permute-start.23 = (bf16[24,1664]{1,0:T(8,128)(2,1)S(1)}, bf16[24,1664]{1,0:T(8,128)(2,1)S(1)}, u32[]{:S(2)}, u32[]{:S(2)}) collective-permute-start(bf16[24,1664]{1,0:T(8,128)(2,1)S(1)} %fusion.66), channel_id=1, source_target_pairs={{0,1},{1,0},{2,3},{3,2},{4,5},{5,4},{6,7},{7,6},{8,9},{9,8},{10,11... | collective-permute-start | bytes 239624 | tf_op jit(solution)/shard_map/ppermute | solution.py:64
  (315 shorter events, 74.7 us)
Async XLA Ops:
  1.6 10.2 %collective-permute-start.12 = (bf16[48,768]{1,0:T(8,128)(2,1)S(1)}, bf16[48,768]{1,0:T(8,128)(2,1)S(1)}, u32[]{:S(2)}, u32[]{:S(2)}) collective-permute-start(bf16[48,768]{1,0:T(8,128)(2,1)S(1)} %broadcast_select_fusion.2), channel_id=1, source_target_pairs={{0,1},{1,0},{2,3},{3,2},{4,5},{5,4},{6,7},{7,6},{8,9},{9,8},{10,11... | collective-permute-start | bytes 221192 | tf_op jit(solution)/shard_map/ppermute | solution.py:64
  3.1 8.7 %collective-permute-start.6 = (bf16[24,1536]{1,0:T(8,128)(2,1)S(1)}, bf16[24,1536]{1,0:T(8,128)(2,1)S(1)}, u32[]{:S(2)}, u32[]{:S(2)}) collective-permute-start(bf16[24,1536]{1,0:T(8,128)(2,1)S(1)} %broadcast_select_fusion.4), channel_id=1, source_target_pairs={{0,1},{1,0},{2,3},{3,2},{4,5},{5,4},{6,7},{7,6},{8,9},{9,8},{10,11... | collective-permute-start | bytes 221192 | tf_op jit(solution)/shard_map/ppermute | solution.py:64
  4.8 11.3 %collective-permute-start = (bf16[24,1664]{1,0:T(8,128)(2,1)S(1)}, bf16[24,1664]{1,0:T(8,128)(2,1)S(1)}, u32[]{:S(2)}, u32[]{:S(2)}) collective-permute-start(bf16[24,1664]{1,0:T(8,128)(2,1)S(1)} %broadcast_select_fusion), channel_id=1, source_target_pairs={{0,1},{1,0},{2,3},{3,2},{4,5},{5,4},{6,7},{7,6},{8,9},{9,8},{10,11... | collective-permute-start | bytes 239624 | tf_op jit(solution)/shard_map/ppermute | solution.py:64
  8.0 8.1 %copy-start.44 = (bf16[24,768]{1,0:T(8,128)(2,1)S(1)}, bf16[24,768]{1,0:T(8,128)(2,1)}, u32[]{:S(2)}) copy-start(bf16[24,768]{1,0:T(8,128)(2,1)} %param.21) | copy-start | bytes 110596
  8.0 8.1 %copy-start.45 = (bf16[24,768]{1,0:T(8,128)(2,1)S(1)}, bf16[24,768]{1,0:T(8,128)(2,1)}, u32[]{:S(2)}) copy-start(bf16[24,768]{1,0:T(8,128)(2,1)} %param.20) | copy-start | bytes 110596
  11.2 124.9 %copy-start.19 = (bf16[256,768]{1,0:T(8,128)(2,1)}, bf16[256,768]{1,0:T(8,128)(2,1)S(1)}, u32[]{:S(2)}) copy-start(bf16[256,768]{1,0:T(8,128)(2,1)S(1)} %get-tuple-element.66) | copy-start | bytes 1179652
  11.2 97.7 %copy-start.52 = (f32[256]{0:T(256)}, f32[256]{0:T(256)S(1)}, u32[]{:S(2)}) copy-start(f32[256]{0:T(256)S(1)} %fusion.71) | copy-start | bytes 3076
  11.9 13.5 %collective-permute-start.13 = (bf16[1,2,48,768]{3,2,1,0:T(8,128)(2,1)S(1)}, bf16[1,2,48,768]{3,2,1,0:T(8,128)(2,1)S(1)}, u32[]{:S(2)}, u32[]{:S(2)}) collective-permute-start(bf16[1,2,48,768]{3,2,1,0:T(8,128)(2,1)S(1)} %maximum_bitcast_fusion), channel_id=1, source_target_pairs={{0,16},{1,17},{2,18},{3,19},{4,20},{5,21},{6,22},{7,23},{8,24},{9,... | collective-permute-start | bytes 442376 | tf_op jit(solution)/shard_map/ppermute | solution.py:64
  14.5 9.3 %collective-permute-start.7 = (bf16[1,2,24,1536]{3,2,1,0:T(8,128)(2,1)S(1)}, bf16[1,2,24,1536]{3,2,1,0:T(8,128)(2,1)S(1)}, u32[]{:S(2)}, u32[]{:S(2)}) collective-permute-start(bf16[1,2,24,1536]{3,2,1,0:T(8,128)(2,1)S(1)} %get-tuple-element.63), channel_id=1, source_target_pairs={{0,2},{1,5},{2,0},{3,7},{4,6},{5,1},{6,4},{7,3},{8,10},{9,13},{10,... | collective-permute-start | bytes 442376 | tf_op jit(solution)/shard_map/ppermute | solution.py:64
  16.2 9.8 %collective-permute-start.1 = (bf16[1,2,24,1664]{3,2,1,0:T(8,128)(2,1)S(1)}, bf16[1,2,24,1664]{3,2,1,0:T(8,128)(2,1)S(1)}, u32[]{:S(2)}, u32[]{:S(2)}) collective-permute-start(bf16[1,2,24,1664]{3,2,1,0:T(8,128)(2,1)S(1)} %get-tuple-element.61), channel_id=1, source_target_pairs={{0,4},{1,3},{2,6},{3,1},{4,0},{5,7},{6,2},{7,5},{8,12},{9,11},{10,... | collective-permute-start | bytes 479240 | tf_op jit(solution)/shard_map/ppermute | solution.py:64
  23.8 12.3 %collective-permute-start.8 = (bf16[2,2,24,1536]{3,2,1,0:T(8,128)(2,1)S(1)}, bf16[2,2,24,1536]{3,2,1,0:T(8,128)(2,1)S(1)}, u32[]{:S(2)}, u32[]{:S(2)}) collective-permute-start(bf16[2,2,24,1536]{3,2,1,0:T(8,128)(2,1)S(1)} %pad_maximum_fusion.7), channel_id=1, source_target_pairs={{0,8},{1,17},{2,10},{3,19},{4,12},{5,21},{6,14},{7,23},{8,0},{9,25... | collective-permute-start | bytes 884744 | tf_op jit(solution)/shard_map/ppermute | solution.py:64
  25.4 8.4 %collective-permute-start.14 = (bf16[2,2,48,768]{3,2,1,0:T(8,128)(2,1)S(1)}, bf16[2,2,48,768]{3,2,1,0:T(8,128)(2,1)S(1)}, u32[]{:S(2)}, u32[]{:S(2)}) collective-permute-start(bf16[2,2,48,768]{3,2,1,0:T(8,128)(2,1)S(1)} %pad_maximum_fusion.8), channel_id=1, source_target_pairs={{0,8},{1,5},{2,10},{3,7},{4,12},{5,1},{6,14},{7,3},{8,0},{9,13},{1... | collective-permute-start | bytes 884744 | tf_op jit(solution)/shard_map/ppermute | solution.py:64
  26.1 9.6 %collective-permute-start.2 = (bf16[2,2,24,1664]{3,2,1,0:T(8,128)(2,1)S(1)}, bf16[2,2,24,1664]{3,2,1,0:T(8,128)(2,1)S(1)}, u32[]{:S(2)}, u32[]{:S(2)}) collective-permute-start(bf16[2,2,24,1664]{3,2,1,0:T(8,128)(2,1)S(1)} %pad_maximum_fusion.6), channel_id=1, source_target_pairs={{0,2},{1,5},{2,0},{3,7},{4,6},{5,1},{6,4},{7,3},{8,10},{9,13},{10,... | collective-permute-start | bytes 958472 | tf_op jit(solution)/shard_map/ppermute | solution.py:64
  33.9 18.4 %collective-permute-start.15 = (bf16[4,2,48,768]{3,2,1,0:T(8,128)(2,1)S(1)}, bf16[4,2,48,768]{3,2,1,0:T(8,128)(2,1)S(1)}, u32[]{:S(2)}, u32[]{:S(2)}) collective-permute-start(bf16[4,2,48,768]{3,2,1,0:T(8,128)(2,1)S(1)} %pad_maximum_fusion.5), channel_id=1, source_target_pairs={{0,4},{1,3},{2,6},{3,1},{4,0},{5,7},{6,2},{7,5},{8,12},{9,11},{10,... | collective-permute-start | bytes 1769480 | tf_op jit(solution)/shard_map/ppermute | solution.py:64
  35.8 18.2 %collective-permute-start.3 = (bf16[4,2,24,1664]{3,2,1,0:T(8,128)(2,1)S(1)}, bf16[4,2,24,1664]{3,2,1,0:T(8,128)(2,1)S(1)}, u32[]{:S(2)}, u32[]{:S(2)}) collective-permute-start(bf16[4,2,24,1664]{3,2,1,0:T(8,128)(2,1)S(1)} %pad_maximum_fusion.3), channel_id=1, source_target_pairs={{0,16},{1,9},{2,18},{3,11},{4,20},{5,13},{6,22},{7,15},{8,24},{9,1... | collective-permute-start | bytes 1916936 | tf_op jit(solution)/shard_map/ppermute | solution.py:64
  36.2 28.1 %collective-permute-start.9 = (bf16[4,2,24,1536]{3,2,1,0:T(8,128)(2,1)S(1)}, bf16[4,2,24,1536]{3,2,1,0:T(8,128)(2,1)S(1)}, u32[]{:S(2)}, u32[]{:S(2)}) collective-permute-start(bf16[4,2,24,1536]{3,2,1,0:T(8,128)(2,1)S(1)} %pad_maximum_fusion.4), channel_id=1, source_target_pairs={{0,4},{1,3},{2,6},{3,1},{4,0},{5,7},{6,2},{7,5},{8,12},{9,11},{10,... | collective-permute-start | bytes 1769480 | tf_op jit(solution)/shard_map/ppermute | solution.py:64
  52.4 22.7 %collective-permute-start.16 = (bf16[8,2,48,768]{3,2,1,0:T(8,128)(2,1)S(1)}, bf16[8,2,48,768]{3,2,1,0:T(8,128)(2,1)S(1)}, u32[]{:S(2)}, u32[]{:S(2)}) collective-permute-start(bf16[8,2,48,768]{3,2,1,0:T(8,128)(2,1)S(1)} %pad_maximum_fusion.2), channel_id=1, source_target_pairs={{0,2},{1,9},{2,0},{3,11},{4,6},{5,13},{6,4},{7,15},{8,10},{9,1},{1... | collective-permute-start | bytes 3538952 | tf_op jit(solution)/shard_map/ppermute | solution.py:64
  54.1 31.0 %collective-permute-start.4 = (bf16[8,2,24,1664]{3,2,1,0:T(8,128)(2,1)S(1)}, bf16[8,2,24,1664]{3,2,1,0:T(8,128)(2,1)S(1)}, u32[]{:S(2)}, u32[]{:S(2)}) collective-permute-start(bf16[8,2,24,1664]{3,2,1,0:T(8,128)(2,1)S(1)} %pad_maximum_fusion), channel_id=1, source_target_pairs={{0,8},{1,17},{2,10},{3,19},{4,12},{5,21},{6,14},{7,23},{8,0},{9,25... | collective-permute-start | bytes 3833864 | tf_op jit(solution)/shard_map/ppermute | solution.py:64
  64.4 21.0 %collective-permute-start.10 = (bf16[8,2,24,1536]{3,2,1,0:T(8,128)(2,1)S(1)}, bf16[8,2,24,1536]{3,2,1,0:T(8,128)(2,1)S(1)}, u32[]{:S(2)}, u32[]{:S(2)}) collective-permute-start(bf16[8,2,24,1536]{3,2,1,0:T(8,128)(2,1)S(1)} %pad_maximum_fusion.1), channel_id=1, source_target_pairs={{0,16},{1,9},{2,18},{3,11},{4,20},{5,13},{6,22},{7,15},{8,24},{9,1... | collective-permute-start | bytes 3538952 | tf_op jit(solution)/shard_map/ppermute | solution.py:64
  75.2 15.2 %collective-permute-start.17 = (bf16[16,2,48,768]{3,2,1,0:T(8,128)(2,1)S(1)}, bf16[16,2,48,768]{3,2,1,0:T(8,128)(2,1)S(1)}, u32[]{:S(2)}, u32[]{:S(2)}) collective-permute-start(bf16[16,2,48,768]{3,2,1,0:T(8,128)(2,1)S(1)} %constant_dynamic-update-slice_fusion.18), channel_id=1, source_target_pairs={{0,1},{1,0},{2,3},{3,2},{4,5},{5,4},{6,7},{7,6},{8,9},{9,8},{10,11... | collective-permute-start | bytes 7077896 | tf_op jit(solution)/shard_map/ppermute | solution.py:64
  85.3 18.2 %collective-permute-start.5 = (bf16[16,2,24,1664]{3,2,1,0:T(8,128)(2,1)S(1)}, bf16[16,2,24,1664]{3,2,1,0:T(8,128)(2,1)S(1)}, u32[]{:S(2)}, u32[]{:S(2)}) collective-permute-start(bf16[16,2,24,1664]{3,2,1,0:T(8,128)(2,1)S(1)} %constant_dynamic-update-slice_fusion.4), channel_id=1, source_target_pairs={{0,1},{1,0},{2,3},{3,2},{4,5},{5,4},{6,7},{7,6},{8,9},{9,8},{10,11... | collective-permute-start | bytes 7667720 | tf_op jit(solution)/shard_map/ppermute | solution.py:64
  85.5 14.0 %collective-permute-start.11 = (bf16[16,2,24,1536]{3,2,1,0:T(8,128)(2,1)S(1)}, bf16[16,2,24,1536]{3,2,1,0:T(8,128)(2,1)S(1)}, u32[]{:S(2)}, u32[]{:S(2)}) collective-permute-start(bf16[16,2,24,1536]{3,2,1,0:T(8,128)(2,1)S(1)} %constant_dynamic-update-slice_fusion.13), channel_id=1, source_target_pairs={{0,1},{1,0},{2,3},{3,2},{4,5},{5,4},{6,7},{7,6},{8,9},{9,8},{10,11... | collective-permute-start | bytes 7077896 | tf_op jit(solution)/shard_map/ppermute | solution.py:64
  111.5 9.0 %copy-start.26 = (bf16[256,768]{0,1:T(8,128)(2,1)}, bf16[256,768]{0,1:T(8,128)(2,1)S(1)}, u32[]{:S(2)}) copy-start(bf16[256,768]{0,1:T(8,128)(2,1)S(1)} %copy.78) | copy-start | bytes 1179652
  124.9 13.3 %copy-start.22 = (f32[256,768]{1,0:T(8,128)}, f32[256,768]{1,0:T(8,128)S(1)}, u32[]{:S(2)}) copy-start(f32[256,768]{1,0:T(8,128)S(1)} %get-tuple-element.70) | copy-start | bytes 2359300
  124.9 13.3 %copy-start.46 = (f32[256]{0:T(256)}, f32[256]{0:T(256)S(1)}, u32[]{:S(2)}) copy-start(f32[256]{0:T(256)S(1)} %fusion.72) | copy-start | bytes 3076
  153.6 8.6 %copy-start.62 = (bf16[256]{0:T(256)(128)(2,1)S(1)}, bf16[256]{0:T(256)(128)(2,1)}, u32[]{:S(2)}) copy-start(bf16[256]{0:T(256)(128)(2,1)} %get-tuple-element.43) | copy-start | bytes 1540
  153.6 9.0 %copy-start.27 = (bf16[256,768]{0,1:T(8,128)(2,1)S(1)}, bf16[256,768]{0,1:T(8,128)(2,1)}, u32[]{:S(2)}) copy-start(bf16[256,768]{0,1:T(8,128)(2,1)} %copy-done.26) | copy-start | bytes 1179652
  153.9 9.1 %copy-start.5 = (bf16[768,768]{1,0:T(8,128)(2,1)S(1)}, bf16[768,768]{1,0:T(8,128)(2,1)}, u32[]{:S(2)}) copy-start(bf16[768,768]{1,0:T(8,128)(2,1)} %copy-done.4) | copy-start | bytes 3538948
  153.9 9.2 %copy-start.20 = (bf16[256,768]{1,0:T(8,128)(2,1)S(1)}, bf16[256,768]{1,0:T(8,128)(2,1)}, u32[]{:S(2)}) copy-start(bf16[256,768]{1,0:T(8,128)(2,1)} %copy-done.19) | copy-start | bytes 1179652
  153.9 9.2 %copy-start.53 = (f32[256]{0:T(256)S(1)}, f32[256]{0:T(256)}, u32[]{:S(2)}) copy-start(f32[256]{0:T(256)} %copy-done.52) | copy-start | bytes 3076
  153.9 39.8 %collective-permute-start.24 = (bf16[16,2,24,1536]{3,2,1,0:T(8,128)(2,1)}, bf16[16,2,24,1536]{3,2,1,0:T(8,128)(2,1)}, u32[]{:S(2)}, u32[]{:S(2)}) collective-permute-start(bf16[16,2,24,1536]{3,2,1,0:T(8,128)(2,1)} %bitcast.65), channel_id=1, source_target_pairs={{0,1},{1,0},{2,3},{3,2},{4,5},{5,4},{6,7},{7,6},{8,9},{9,8},{10,11... | collective-permute-start | bytes 7077896 | tf_op jit(solution)/shard_map/ppermute | solution.py:64
  162.2 36.6 %collective-permute-start.30 = (bf16[16,2,48,768]{3,2,1,0:T(8,128)(2,1)}, bf16[16,2,48,768]{3,2,1,0:T(8,128)(2,1)}, u32[]{:S(2)}, u32[]{:S(2)}) collective-permute-start(bf16[16,2,48,768]{3,2,1,0:T(8,128)(2,1)} %bitcast.69), channel_id=1, source_target_pairs={{0,1},{1,0},{2,3},{3,2},{4,5},{5,4},{6,7},{7,6},{8,9},{9,8},{10,11... | collective-permute-start | bytes 7077896 | tf_op jit(solution)/shard_map/ppermute | solution.py:64
  187.4 19.5 %collective-permute-start.18 = (bf16[16,2,24,1664]{3,2,1,0:T(8,128)(2,1)S(1)}, bf16[16,2,24,1664]{3,2,1,0:T(8,128)(2,1)S(1)}, u32[]{:S(2)}, u32[]{:S(2)}) collective-permute-start(bf16[16,2,24,1664]{3,2,1,0:T(8,128)(2,1)S(1)} %bitcast.179), channel_id=1, source_target_pairs={{0,1},{1,0},{2,3},{3,2},{4,5},{5,4},{6,7},{7,6},{8,9},{9,8},{10,11... | collective-permute-start | bytes 7667720 | tf_op jit(solution)/shard_map/ppermute | solution.py:64
  196.2 25.0 %collective-permute-start.25 = (bf16[8,2,24,1536]{3,2,1,0:T(8,128)(2,1)S(1)}, bf16[8,2,24,1536]{3,2,1,0:T(8,128)(2,1)S(1)}, u32[]{:S(2)}, u32[]{:S(2)}) collective-permute-start(bf16[8,2,24,1536]{3,2,1,0:T(8,128)(2,1)S(1)} %slice.329), channel_id=1, source_target_pairs={{0,16},{1,9},{2,18},{3,11},{4,20},{5,13},{6,22},{7,15},{8,24},{9,1... | collective-permute-start | bytes 3538952 | tf_op jit(solution)/shard_map/ppermute | solution.py:64
  201.3 24.6 %collective-permute-start.31 = (bf16[8,2,48,768]{3,2,1,0:T(8,128)(2,1)S(1)}, bf16[8,2,48,768]{3,2,1,0:T(8,128)(2,1)S(1)}, u32[]{:S(2)}, u32[]{:S(2)}) collective-permute-start(bf16[8,2,48,768]{3,2,1,0:T(8,128)(2,1)S(1)} %slice.328), channel_id=1, source_target_pairs={{0,2},{1,9},{2,0},{3,11},{4,6},{5,13},{6,4},{7,15},{8,10},{9,1},{1... | collective-permute-start | bytes 3538952 | tf_op jit(solution)/shard_map/ppermute | solution.py:64
  207.6 30.6 %collective-permute-start.19 = (bf16[8,2,24,1664]{3,2,1,0:T(8,128)(2,1)S(1)}, bf16[8,2,24,1664]{3,2,1,0:T(8,128)(2,1)S(1)}, u32[]{:S(2)}, u32[]{:S(2)}) collective-permute-start(bf16[8,2,24,1664]{3,2,1,0:T(8,128)(2,1)S(1)} %slice.327), channel_id=1, source_target_pairs={{0,8},{1,17},{2,10},{3,19},{4,12},{5,21},{6,14},{7,23},{8,0},{9,25... | collective-permute-start | bytes 3833864 | tf_op jit(solution)/shard_map/ppermute | solution.py:64
  221.7 24.8 %collective-permute-start.26 = (bf16[4,2,24,1536]{3,2,1,0:T(8,128)(2,1)S(1)}, bf16[4,2,24,1536]{3,2,1,0:T(8,128)(2,1)S(1)}, u32[]{:S(2)}, u32[]{:S(2)}) collective-permute-start(bf16[4,2,24,1536]{3,2,1,0:T(8,128)(2,1)S(1)} %slice.332), channel_id=1, source_target_pairs={{0,4},{1,3},{2,6},{3,1},{4,0},{5,7},{6,2},{7,5},{8,12},{9,11},{10,... | collective-permute-start | bytes 1769480 | tf_op jit(solution)/shard_map/ppermute | solution.py:64
  226.2 26.6 %collective-permute-start.32 = (bf16[4,2,48,768]{3,2,1,0:T(8,128)(2,1)S(1)}, bf16[4,2,48,768]{3,2,1,0:T(8,128)(2,1)S(1)}, u32[]{:S(2)}, u32[]{:S(2)}) collective-permute-start(bf16[4,2,48,768]{3,2,1,0:T(8,128)(2,1)S(1)} %slice.331), channel_id=1, source_target_pairs={{0,4},{1,3},{2,6},{3,1},{4,0},{5,7},{6,2},{7,5},{8,12},{9,11},{10,... | collective-permute-start | bytes 1769480 | tf_op jit(solution)/shard_map/ppermute | solution.py:64
  238.5 23.8 %collective-permute-start.20 = (bf16[4,2,24,1664]{3,2,1,0:T(8,128)(2,1)S(1)}, bf16[4,2,24,1664]{3,2,1,0:T(8,128)(2,1)S(1)}, u32[]{:S(2)}, u32[]{:S(2)}) collective-permute-start(bf16[4,2,24,1664]{3,2,1,0:T(8,128)(2,1)S(1)} %slice.330), channel_id=1, source_target_pairs={{0,16},{1,9},{2,18},{3,11},{4,20},{5,13},{6,22},{7,15},{8,24},{9,1... | collective-permute-start | bytes 1916936 | tf_op jit(solution)/shard_map/ppermute | solution.py:64
  246.7 7.8 %collective-permute-start.27 = (bf16[2,2,24,1536]{3,2,1,0:T(8,128)(2,1)S(1)}, bf16[2,2,24,1536]{3,2,1,0:T(8,128)(2,1)S(1)}, u32[]{:S(2)}, u32[]{:S(2)}) collective-permute-start(bf16[2,2,24,1536]{3,2,1,0:T(8,128)(2,1)S(1)} %slice.335), channel_id=1, source_target_pairs={{0,8},{1,17},{2,10},{3,19},{4,12},{5,21},{6,14},{7,23},{8,0},{9,25... | collective-permute-start | bytes 884744 | tf_op jit(solution)/shard_map/ppermute | solution.py:64
  253.0 6.8 %collective-permute-start.33 = (bf16[2,2,48,768]{3,2,1,0:T(8,128)(2,1)S(1)}, bf16[2,2,48,768]{3,2,1,0:T(8,128)(2,1)S(1)}, u32[]{:S(2)}, u32[]{:S(2)}) collective-permute-start(bf16[2,2,48,768]{3,2,1,0:T(8,128)(2,1)S(1)} %slice.334), channel_id=1, source_target_pairs={{0,8},{1,5},{2,10},{3,7},{4,12},{5,1},{6,14},{7,3},{8,0},{9,13},{1... | collective-permute-start | bytes 884744 | tf_op jit(solution)/shard_map/ppermute | solution.py:64
  254.6 10.7 %collective-permute-start.28 = (bf16[1,2,24,1536]{3,2,1,0:T(8,128)(2,1)S(1)}, bf16[1,2,24,1536]{3,2,1,0:T(8,128)(2,1)S(1)}, u32[]{:S(2)}, u32[]{:S(2)}) collective-permute-start(bf16[1,2,24,1536]{3,2,1,0:T(8,128)(2,1)S(1)} %slice.338), channel_id=1, source_target_pairs={{0,2},{1,5},{2,0},{3,7},{4,6},{5,1},{6,4},{7,3},{8,10},{9,13},{10,... | collective-permute-start | bytes 442376 | tf_op jit(solution)/shard_map/ppermute | solution.py:64
  259.9 13.1 %collective-permute-start.34 = (bf16[1,2,48,768]{3,2,1,0:T(8,128)(2,1)S(1)}, bf16[1,2,48,768]{3,2,1,0:T(8,128)(2,1)S(1)}, u32[]{:S(2)}, u32[]{:S(2)}) collective-permute-start(bf16[1,2,48,768]{3,2,1,0:T(8,128)(2,1)S(1)} %slice.337), channel_id=1, source_target_pairs={{0,16},{1,17},{2,18},{3,19},{4,20},{5,21},{6,22},{7,23},{8,24},{9,... | collective-permute-start | bytes 442376 | tf_op jit(solution)/shard_map/ppermute | solution.py:64
  262.5 13.3 %collective-permute-start.21 = (bf16[2,2,24,1664]{3,2,1,0:T(8,128)(2,1)S(1)}, bf16[2,2,24,1664]{3,2,1,0:T(8,128)(2,1)S(1)}, u32[]{:S(2)}, u32[]{:S(2)}) collective-permute-start(bf16[2,2,24,1664]{3,2,1,0:T(8,128)(2,1)S(1)} %slice.333), channel_id=1, source_target_pairs={{0,2},{1,5},{2,0},{3,7},{4,6},{5,1},{6,4},{7,3},{8,10},{9,13},{10,... | collective-permute-start | bytes 958472 | tf_op jit(solution)/shard_map/ppermute | solution.py:64
  265.4 9.6 %collective-permute-start.29 = (bf16[24,1536]{1,0:T(8,128)(2,1)S(1)}, bf16[24,1536]{1,0:T(8,128)(2,1)S(1)}, u32[]{:S(2)}, u32[]{:S(2)}) collective-permute-start(bf16[24,1536]{1,0:T(8,128)(2,1)S(1)} %fusion.69), channel_id=1, source_target_pairs={{0,1},{1,0},{2,3},{3,2},{4,5},{5,4},{6,7},{7,6},{8,9},{9,8},{10,11... | collective-permute-start | bytes 221192 | tf_op jit(solution)/shard_map/ppermute | solution.py:64
  273.1 4.5 %collective-permute-start.35 = (bf16[48,768]{1,0:T(8,128)(2,1)S(1)}, bf16[48,768]{1,0:T(8,128)(2,1)S(1)}, u32[]{:S(2)}, u32[]{:S(2)}) collective-permute-start(bf16[48,768]{1,0:T(8,128)(2,1)S(1)} %fusion.70), channel_id=1, source_target_pairs={{0,1},{1,0},{2,3},{3,2},{4,5},{5,4},{6,7},{7,6},{8,9},{9,8},{10,11... | collective-permute-start | bytes 221192 | tf_op jit(solution)/shard_map/ppermute | solution.py:64
  275.9 10.0 %collective-permute-start.22 = (bf16[1,2,24,1664]{3,2,1,0:T(8,128)(2,1)S(1)}, bf16[1,2,24,1664]{3,2,1,0:T(8,128)(2,1)S(1)}, u32[]{:S(2)}, u32[]{:S(2)}) collective-permute-start(bf16[1,2,24,1664]{3,2,1,0:T(8,128)(2,1)S(1)} %slice.336), channel_id=1, source_target_pairs={{0,4},{1,3},{2,6},{3,1},{4,0},{5,7},{6,2},{7,5},{8,12},{9,11},{10,... | collective-permute-start | bytes 479240 | tf_op jit(solution)/shard_map/ppermute | solution.py:64
  285.9 4.8 %collective-permute-start.23 = (bf16[24,1664]{1,0:T(8,128)(2,1)S(1)}, bf16[24,1664]{1,0:T(8,128)(2,1)S(1)}, u32[]{:S(2)}, u32[]{:S(2)}) collective-permute-start(bf16[24,1664]{1,0:T(8,128)(2,1)S(1)} %fusion.66), channel_id=1, source_target_pairs={{0,1},{1,0},{2,3},{3,2},{4,5},{5,4},{6,7},{7,6},{8,9},{9,8},{10,11... | collective-permute-start | bytes 239624 | tf_op jit(solution)/shard_map/ppermute | solution.py:64
  (59 other events, 205.8 us)
